TPU v7x, 512 devices: a whole 4x8x8 slice. The times are simulated.
512 devices in a mesh: img: 16 (over z, core), proto: 32 (over x, y).
Axes of the slice: x: 4, y: 8, z: 8, core: 2. Of those that a mesh axis runs over, the one named last changes fastest.
Arguments:
- images: bfloat16 [32768, 256], P('img'), may hold values from -24 to 24
- prototypes: bfloat16 [131072, 256], P('proto'), may hold values from -24 to 24
- tile_row: int32 [16, 32, 6], P('img', 'proto'), may hold values from 0 to 3
- tile_proto: int32 [16, 32, 6], P('img', 'proto'), may hold values from 0 to 7
- tile_valid: int32 [16, 32, 6], P('img', 'proto'), may hold values from 0 to 1, as said below
Outputs:
- proto_sums: float32 [131072, 256], P(('proto', 'img'))
- col_potential: float32 [131072], P('proto')
Inputs may be any that keep to these rules, and one draw needn't show every extreme that they name: `tile_valid`: on every device the valid slots come before the padded ones, at least one slot is valid, and the valid slots name distinct (row block, prototype block) pairs; some device has all 6 slots valid. Every row block has a valid slot on some device of its img index, and every prototype block on some device of its proto index.
All inputs are finite; a program needn't handle non-finite values.
Results may differ from a plain program's by a relative error of at most 0.012.
Values may be sent and summed in bfloat16 or wider, within the bound.
A program may use at most 64 MiB of HBM per device.

v0:
```python
import math

import jax
import jax.numpy as jnp
from jax import lax
from jax.sharding import PartitionSpec as P

E = 256
TILE = 512
RB_DEV = 4
PB_DEV = 8
MAXT = 6
ITERS = 3


far_below = -1e30


def running_top(values_of, live_slots, reduced, slot_blocks, block_count):

    def advance(position, tops):
        local_top = jnp.max(values_of(position), axis=reduced)
        target = slot_blocks[position]
        old_top = lax.dynamic_index_in_dim(tops, target, 0, keepdims=False)
        return lax.dynamic_update_index_in_dim(tops, jnp.maximum(old_top, local_top), target, 0)

    return lax.fori_loop(
        0, live_slots, advance, jnp.full((block_count, TILE), far_below, jnp.float32)
    )


def running_mass(values_of, live_slots, reduced, slot_blocks, tops):

    def advance(position, masses):
        target = slot_blocks[position]
        top_here = lax.dynamic_index_in_dim(tops, target, 0, keepdims=False)
        local_mass = jnp.sum(
            jnp.exp(values_of(position) - jnp.expand_dims(top_here, reduced)), axis=reduced
        )
        old_mass = lax.dynamic_index_in_dim(masses, target, 0, keepdims=False)
        return lax.dynamic_update_index_in_dim(masses, old_mass + local_mass, target, 0)

    return lax.fori_loop(0, live_slots, advance, jnp.zeros_like(tops))


def shards(images, prototypes, tile_row, tile_proto, tile_valid):
    img_count = lax.axis_size("img")
    proto_count = lax.axis_size("proto")
    image_blocks = images.reshape(RB_DEV, TILE, E)
    proto_blocks = prototypes.reshape(PB_DEV, TILE, E)
    slot_rows = tile_row.reshape(MAXT)
    slot_protos = tile_proto.reshape(MAXT)
    live_slots = jnp.sum(tile_valid)
    score_scale = float(E) ** (-0.5)
    log_ratio = math.log(PB_DEV * proto_count / (RB_DEV * img_count))

    def fresh_scores(position):
        rows_here = lax.dynamic_index_in_dim(image_blocks, slot_rows[position], 0, keepdims=False)
        protos_here = lax.dynamic_index_in_dim(
            proto_blocks, slot_protos[position], 0, keepdims=False
        )
        products = lax.dot_general(
            rows_here, protos_here, (((1,), (1,)), ((), ())), preferred_element_type=jnp.float32
        )
        return products * score_scale

    def fill_cache(position, cache):
        return lax.dynamic_update_index_in_dim(cache, fresh_scores(position), position, 0)

    score_cache = lax.fori_loop(
        0, live_slots, fill_cache, jnp.zeros((MAXT, TILE, TILE), jnp.float32)
    )

    def scores_at(position):
        return lax.dynamic_index_in_dim(score_cache, position, 0, keepdims=False)

    col_pot = jnp.zeros((PB_DEV, TILE), jnp.float32)
    row_pot = jnp.zeros((RB_DEV, TILE), jnp.float32)
    for iteration in range(ITERS):

        def row_values_of(position):
            return scores_at(position) + lax.dynamic_index_in_dim(
                col_pot, slot_protos[position], 0, keepdims=True
            )

        row_highest = lax.pmax(
            running_top(row_values_of, live_slots, 1, slot_rows, RB_DEV), "proto"
        )
        row_summed = lax.psum(
            running_mass(row_values_of, live_slots, 1, slot_rows, row_highest), "proto"
        )
        row_pot = log_ratio - (row_highest + jnp.log(row_summed))

        def values_of(position):
            return (
                scores_at(position)
                + lax.dynamic_index_in_dim(row_pot, slot_rows[position], 0, keepdims=False)[:, None]
            )

        highest = lax.pmax(running_top(values_of, live_slots, 0, slot_protos, PB_DEV), "img")
        summed = lax.psum(running_mass(values_of, live_slots, 0, slot_protos, highest), "img")
        col_pot = -(highest + jnp.log(summed))

    def tile_term(position):
        target = slot_protos[position]
        source = slot_rows[position]
        shifted = (
            scores_at(position)
            + lax.dynamic_index_in_dim(row_pot, source, 0, keepdims=False)[:, None]
        )
        weights = jnp.exp(
            shifted + lax.dynamic_index_in_dim(col_pot, target, 0, keepdims=True)
        ).astype(jnp.bfloat16)
        rows_here = lax.dynamic_index_in_dim(image_blocks, source, 0, keepdims=False)
        return lax.dot_general(
            weights, rows_here, (((0,), (0,)), ((), ())), preferred_element_type=jnp.float32
        )

    def add_tile(position, partial_value):
        target = slot_protos[position]
        current = lax.dynamic_index_in_dim(partial_value, target, 0, keepdims=False)
        return lax.dynamic_update_index_in_dim(
            partial_value, current + tile_term(position), target, 0
        )

    partial_value = lax.fori_loop(
        0, live_slots, add_tile, jnp.zeros((PB_DEV, TILE, E), jnp.float32)
    )
    proto_share = lax.psum_scatter(
        partial_value.reshape(PB_DEV * TILE, E).astype(jnp.bfloat16),
        "img",
        scatter_dimension=0,
        tiled=True,
    ).astype(jnp.float32)
    return (proto_share, col_pot.reshape(PB_DEV * TILE))


def solution(mesh):
    return jax.shard_map(
        shards,
        mesh=mesh,
        in_specs=(
            P("img", None),
            P("proto", None),
            P("img", "proto", None),
            P("img", "proto", None),
            P("img", "proto", None),
        ),
        out_specs=(P(("proto", "img"), None), P("proto")),
        check_vma=False,
    )
```

profile of v0, /device:TPU:1, one launch (start us, length us, event | category | flops | bytes accessed | tf_op | source)
XLA Modules:
  0.0 1330.1 jit_solution(14880688892375217846)
XLA Ops:
  7.2 1.4 reduce_sum.76
  8.6 3.5 broadcast_in_dim.42
  12.1 8.7 while.142
  12.8 0.7 dynamic_slice.369
  15.3 0.7 dynamic_slice.368
  17.9 2.3 fusion.57
  20.8 5.3 while.143
  21.5 0.7 dynamic_slice.372
  24.1 1.4 dynamic-slice_reduce_fusion.2
  26.2 119.4 %pmax.42 = f32[4,512]{1,0:T(4,128)S(1)} all-reduce(f32[4,512]{1,0:T(4,128)S(1)} %get-tuple-element.587), channel_id=1, replica_groups=mesh['img'=16,'proto'=32] {'proto'}, use_global_device_ids=true, to_apply=%region_6.7 | all-reduce | flops 2048 | bytes 16384 | tf_op jit(solution)/shard_map/pmax | solution.py:86
  145.6 5.4 while.144
  148.7 1.5 fusion.58
  151.0 74.4 %psum.42 = f32[4,512]{1,0:T(4,128)S(1)} all-reduce(f32[4,512]{1,0:T(4,128)S(1)} %get-tuple-element.588), channel_id=1, replica_groups=mesh['img'=16,'proto'=32] {'proto'}, use_global_device_ids=true, to_apply=%region_10.11 | all-reduce | flops 2048 | bytes 16384 | tf_op jit(solution)/shard_map/psum | solution.py:89
  225.4 7.8 while.145
  228.6 0.6 dynamic_slice.380
  231.1 1.4 fusion.59
  233.2 97.2 %pmax.43 = f32[8,512]{1,0:T(8,128)S(1)} all-reduce(f32[8,512]{1,0:T(8,128)S(1)} %get-tuple-element.589), channel_id=1, replica_groups=mesh['img'=16,'proto'=32] {'img'}, use_global_device_ids=true, to_apply=%region_14.15 | all-reduce | flops 4096 | bytes 32768 | tf_op jit(solution)/shard_map/pmax | solution.py:100
  330.5 7.8 while.146
  336.1 1.5 fusion.60
  338.3 65.1 %psum.43 = f32[8,512]{1,0:T(8,128)S(1)} all-reduce(f32[8,512]{1,0:T(8,128)S(1)} %get-tuple-element.590), channel_id=1, replica_groups=mesh['img'=16,'proto'=32] {'img'}, use_global_device_ids=true, to_apply=%region_18.19 | all-reduce | flops 4096 | bytes 32768 | tf_op jit(solution)/shard_map/psum | solution.py:101
  403.4 7.2 while.147
  408.5 1.4 fusion.61
  410.6 102.7 %pmax.44 = f32[4,512]{1,0:T(4,128)S(1)} all-reduce(f32[4,512]{1,0:T(4,128)S(1)} %get-tuple-element.591), channel_id=1, replica_groups=mesh['img'=16,'proto'=32] {'proto'}, use_global_device_ids=true, to_apply=%region_22.23 | all-reduce | flops 2048 | bytes 16384 | tf_op jit(solution)/shard_map/pmax | solution.py:86
  513.4 8.0 while.148
  516.6 0.6 dynamic_slice.396
  519.1 1.5 fusion.62
  521.4 86.8 %psum.44 = f32[4,512]{1,0:T(4,128)S(1)} all-reduce(f32[4,512]{1,0:T(4,128)S(1)} %get-tuple-element.592), channel_id=1, replica_groups=mesh['img'=16,'proto'=32] {'proto'}, use_global_device_ids=true, to_apply=%region_26.27 | all-reduce | flops 2048 | bytes 16384 | tf_op jit(solution)/shard_map/psum | solution.py:89
  608.2 7.8 while.149
  608.9 0.6 dynamic_slice.401
  611.4 0.7 dynamic_slice.400
  613.9 1.4 fusion.63
  616.0 98.5 %pmax.45 = f32[8,512]{1,0:T(8,128)S(1)} all-reduce(f32[8,512]{1,0:T(8,128)S(1)} %get-tuple-element.593), channel_id=1, replica_groups=mesh['img'=16,'proto'=32] {'img'}, use_global_device_ids=true, to_apply=%region_30.31 | all-reduce | flops 4096 | bytes 32768 | tf_op jit(solution)/shard_map/pmax | solution.py:100
  714.5 8.4 while.150
  715.2 0.7 dynamic_slice.405
  717.9 0.7 dynamic_slice.406
  720.7 1.5 fusion.64
  722.9 67.4 %psum.45 = f32[8,512]{1,0:T(8,128)S(1)} all-reduce(f32[8,512]{1,0:T(8,128)S(1)} %get-tuple-element.594), channel_id=1, replica_groups=mesh['img'=16,'proto'=32] {'img'}, use_global_device_ids=true, to_apply=%region_34.35 | all-reduce | flops 4096 | bytes 32768 | tf_op jit(solution)/shard_map/psum | solution.py:101
  790.3 7.4 while.151
  795.6 1.4 fusion.65
  797.7 103.0 %pmax.46 = f32[4,512]{1,0:T(4,128)S(1)} all-reduce(f32[4,512]{1,0:T(4,128)S(1)} %get-tuple-element.595), channel_id=1, replica_groups=mesh['img'=16,'proto'=32] {'proto'}, use_global_device_ids=true, to_apply=%region_38.39 | all-reduce | flops 2048 | bytes 16384 | tf_op jit(solution)/shard_map/pmax | solution.py:86
  900.8 8.0 while.152
  901.4 0.6 dynamic_slice.415
  904.0 0.6 dynamic_slice.416
  906.5 1.5 fusion.66
  908.8 86.8 %psum.46 = f32[4,512]{1,0:T(4,128)S(1)} all-reduce(f32[4,512]{1,0:T(4,128)S(1)} %get-tuple-element.596), channel_id=1, replica_groups=mesh['img'=16,'proto'=32] {'proto'}, use_global_device_ids=true, to_apply=%region_42.43 | all-reduce | flops 2048 | bytes 16384 | tf_op jit(solution)/shard_map/psum | solution.py:89
  995.6 7.9 while.153
  996.3 0.7 dynamic_slice.421
  998.9 0.7 dynamic_slice.420
  1001.4 1.4 fusion.67
  1003.5 99.0 %pmax.47 = f32[8,512]{1,0:T(8,128)S(1)} all-reduce(f32[8,512]{1,0:T(8,128)S(1)} %get-tuple-element.597), channel_id=1, replica_groups=mesh['img'=16,'proto'=32] {'img'}, use_global_device_ids=true, to_apply=%region_46.47 | all-reduce | flops 4096 | bytes 32768 | tf_op jit(solution)/shard_map/pmax | solution.py:100
  1102.5 8.0 while.154
  1103.2 0.6 dynamic_slice.425
  1105.7 0.6 dynamic_slice.426
  1108.3 1.5 fusion.68
  1110.5 65.6 %psum.47 = f32[8,512]{1,0:T(8,128)S(1)} all-reduce(f32[8,512]{1,0:T(8,128)S(1)} %get-tuple-element.598), channel_id=1, replica_groups=mesh['img'=16,'proto'=32] {'img'}, use_global_device_ids=true, to_apply=%region_50.51 | all-reduce | flops 4096 | bytes 32768 | tf_op jit(solution)/shard_map/psum | solution.py:101
  1176.2 2.4 broadcast_in_dim.41
  1178.5 10.2 while.155
  1179.2 0.6 dynamic_slice.431
  1181.9 1.1 constant_dynamic-slice_fusion.43
  1183.0 0.7 dynamic_slice.432
  1185.6 2.5 fusion.71
  1188.8 3.8 convert_element_type.15
  1193.2 128.4 %reduce-scatter.2.cloned.1.call-done = bf16[256,256]{1,0:T(8,128)(2,1)} async-done(((bf16[4096,256]{1,0:T(8,128)(2,1)}), bf16[256,256]{1,0:T(8,128)(2,1)}) %reduce-scatter.2.cloned.1.call-update) | async-done | bytes 131088 | tf_op jit(solution)/shard_map/reduce_scatter | solution.py:129
  1321.6 1.6 convert_element_type.17
  (72 shorter events, 7.0 us)
Async XLA Ops:
  7.2 4.9 copy-start.2
  7.2 4.9 copy-start.1
  7.2 4.9 copy-start
  7.2 1314.4 %reduce-scatter.2.cloned.1.call-start = ((), (), s32[]{:S(2)}) async-start(), calls=%async_computation.1 | async-start | bytes 2228224 | tf_op jit(solution)/shard_map/reduce_scatter | solution.py:129
Sparse Core Ops, SparseCore 0:
  1192.7 128.8 reduce-scatter.1
where the time goes:
time: 1340 us; the launch traced here: 1330 us
  blocking collectives  1070 us (80%)
  waiting for transfers between devices  128 us (10%)
  loops' own time  67.7 us (5%)
  local copies, waits for them, and re-layouts  24.6 us (2%)
  other arithmetic  24.3 us (2%)
  between operations  14.3 us (1%)
    pmax x3, blocking collectives, shards(): lax.pmax(running_top(row_values_of, live_slots, 1, slot_rows, RB_DEV), 'p...  325 us
    pmax x3, blocking collectives, shards(): lax.pmax(running_top(values_of, live_slots, 0, slot_protos, PB_DEV), 'img')  295 us
    psum x3, blocking collectives, shards(): lax.psum(running_mass(row_values_of, live_slots, 1, slot_rows, row_highes...  248 us
    psum x3, blocking collectives, shards(): lax.psum(running_mass(values_of, live_slots, 0, slot_protos, highest), 'i...  198 us
    reduce_scatter x1, waiting for transfers between devices, shards(): lax.psum_scatter(partial_value.reshape(PB_DEV * TILE, E).astype(jnp.bfloa...  128 us
    another operation x6, loops' own time, running_mass(): return lax.fori_loop(0, live_slots, advance, jnp.zeros_like(tops))  29.2 us
    another operation x6, loops' own time, running_top(): lax.fori_loop(0, live_slots, advance, jnp.full((block_count, TILE), far_b...  28 us
  transfers between devices with their start and end apart: 1, of which 1 were waited for; matrix products, arithmetic and copies ran while one was open for 0% of the time, Pallas kernels for 0%

commit v1 on v0

--- a/solution.py
+++ b/solution.py
@@ -43,6 +43,14 @@
     return lax.fori_loop(0, live_slots, advance, jnp.zeros_like(tops))
 
 
+def merge_tops(local_top, local_mass, axis):
+    gathered = lax.all_gather(jnp.stack([local_top, local_mass]), axis)
+    tops, masses = gathered[:, 0], gathered[:, 1]
+    highest = jnp.max(tops, axis=0)
+    summed = jnp.sum(masses * jnp.exp(tops - highest[None]), axis=0)
+    return highest, summed
+
+
 def shards(images, prototypes, tile_row, tile_proto, tile_valid):
     img_count = lax.axis_size("img")
     proto_count = lax.axis_size("proto")
@@ -83,12 +91,9 @@
                 col_pot, slot_protos[position], 0, keepdims=True
             )
 
-        row_highest = lax.pmax(
-            running_top(row_values_of, live_slots, 1, slot_rows, RB_DEV), "proto"
-        )
-        row_summed = lax.psum(
-            running_mass(row_values_of, live_slots, 1, slot_rows, row_highest), "proto"
-        )
+        row_local_top = running_top(row_values_of, live_slots, 1, slot_rows, RB_DEV)
+        row_local_mass = running_mass(row_values_of, live_slots, 1, slot_rows, row_local_top)
+        row_highest, row_summed = merge_tops(row_local_top, row_local_mass, "proto")
         row_pot = log_ratio - (row_highest + jnp.log(row_summed))
 
         def values_of(position):
@@ -97,8 +102,9 @@
                 + lax.dynamic_index_in_dim(row_pot, slot_rows[position], 0, keepdims=False)[:, None]
             )
 
-        highest = lax.pmax(running_top(values_of, live_slots, 0, slot_protos, PB_DEV), "img")
-        summed = lax.psum(running_mass(values_of, live_slots, 0, slot_protos, highest), "img")
+        local_top = running_top(values_of, live_slots, 0, slot_protos, PB_DEV)
+        local_mass = running_mass(values_of, live_slots, 0, slot_protos, local_top)
+        highest, summed = merge_tops(local_top, local_mass, "img")
         col_pot = -(highest + jnp.log(summed))
 
     def tile_term(position):

time: 1340 us -> 890 us (0.66)
  blocking collectives: 1070 us -> 519 us
  loops' own time: 67.7 us -> 126 us
  other arithmetic: 24.3 us -> 42.6 us
  local copies, waits for them, and re-layouts: 24.6 us -> 42.6 us
    pmax x6 -> x0, blocking collectives: 620 us -> none  [the longest x3 325 us: shards(): lax.pmax(running_top(row_values_of, live_slots, 1, slot_rows, RB_DEV), 'p...]
    all_gather x0 -> x6, blocking collectives: none -> 519 us  [merge_tops(): gathered = lax.all_gather(jnp.stack([local_top, local_mass]), axis)]
    psum x6 -> x0, blocking collectives: 446 us -> none  [the longest x3 248 us: shards(): lax.psum(running_mass(row_values_of, live_slots, 1, slot_rows, row_highes...]
    another operation x6, loops' own time: 29.2 us -> 54.6 us  [running_mass(): return lax.fori_loop(0, live_slots, advance, jnp.zeros_like(tops))]
    another operation x6, loops' own time: 28 us -> 52.1 us  [running_top(): lax.fori_loop(0, live_slots, advance, jnp.full((block_count, TILE), far_b...]
where the time goes in v1:
time: 890 us; the launch traced here: 879 us
  blocking collectives  519 us (58%)
  loops' own time  126 us (14%)
  waiting for transfers between devices  125 us (14%)
  local copies, waits for them, and re-layouts  42.6 us (5%)
  other arithmetic  42.6 us (5%)
  between operations  14.4 us (2%)
  matrix products  9.6 us (1%)
    all_gather x6, blocking collectives, merge_tops(): gathered = lax.all_gather(jnp.stack([local_top, local_mass]), axis)  519 us
    reduce_scatter x1, waiting for transfers between devices, shards(): lax.psum_scatter(partial_value.reshape(PB_DEV * TILE, E).astype(jnp.bfloa...  125 us
    another operation x6, loops' own time, running_mass(): return lax.fori_loop(0, live_slots, advance, jnp.zeros_like(tops))  54.6 us
    another operation x6, loops' own time, running_top(): lax.fori_loop(0, live_slots, advance, jnp.full((block_count, TILE), far_b...  52.1 us
    reduce_sum x12, other arithmetic, advance(): jnp.sum(jnp.exp(values_of(position) - jnp.expand_dims(top_here, reduced))...  18.1 us
  transfers between devices with their start and end apart: 1, of which 1 were waited for; matrix products, arithmetic and copies ran while one was open for 0% of the time, Pallas kernels for 0%

profile of v1, /device:TPU:1, one launch (start us, length us, event | category | flops | bytes accessed | tf_op | source)
XLA Modules:
  0.0 879.2 jit_solution(12652973708331762540)
XLA Ops:
  7.2 1.4 reduce_sum.130
  8.6 3.5 broadcast_in_dim.38
  12.1 16.8 %while.142 = (s32[]{:T(128)}, f32[6,512,512]{2,1,0:T(8,128)}, s32[]{:T(128)}, s32[6]{0:T(128)S(1)}, bf16[4,512,256]{2,1,0:T(8,128)(2,1)S(1)}, /*index=5*/s32[6]{...) while((s32[]{:T(128)}, f32[6,512,512]{2,1,0:T(8,128)}, ...), condition=%wide.region_2.3_spmd, body=%wide.region_1.2_spmd.sunk | while | flops 134479888 | bytes 1573119 | solution.py:78
  15.3 0.7 dynamic_slice.368
  17.9 2.3 fusion.75
  23.4 0.7 dynamic_slice.368
  25.9 2.3 fusion.75
  28.9 10.0 %while.143 = (s32[]{:T(128)}, f32[4,512]{1,0:T(4,128)S(1)}, s32[]{:T(128)}, s32[6]{0:T(128)S(1)}, f32[6,512,512]{2,1,0:T(8,128)}, /*index=5*/s32[]{:T(128)}, s32[]{:T(128)}, s32[]{:T(128)}, s32[]{:T(128)}) while((s32[]{:T(128)}, f32[4,512]{1,0:T(4,128)S(1)}, s32[]{:T(128)}, s32[6]{0:T(128)S(1)}, f32[6,512,512]{2,1,0:T(8,128)}, ...), condition=%wide.region_5.6_spmd, body=%wide.region_3.5_spmd.sunk | while | flops 262152 | bytes 1061049 | solution.py:27
  29.6 0.7 dynamic_slice.372
  32.2 1.4 dynamic-slice_reduce_fusion.2
  34.3 0.7 dynamic_slice.372
  36.9 1.4 dynamic-slice_reduce_fusion.2
  39.0 10.2 %while.144 = (s32[]{:T(128)}, f32[4,512]{1,0:T(4,128)S(1)}, s32[]{:T(128)}, s32[6]{0:T(128)S(1)}, f32[6,512,512]{2,1,0:T(8,128)}, /*index=5*/f32[4,512]{1,0:T(4,...) while((s32[]{:T(128)}, f32[4,512]{1,0:T(4,128)S(1)}, s32[]{:T(128)}, s32[6]{0:T(128)S(1)}, ...), condition=%wide.region_8.9_spmd, body=%wide.region_6.8_spmd.sunk | while | flops 524296 | bytes 1067205 | solution.py:43
  42.2 1.5 fusion.76
  46.9 1.5 fusion.76
  49.2 106.8 %all-gather = f32[64,4,512]{2,1,0:T(4,128)S(1)} all-gather(f32[2,4,512]{2,1,0:T(4,128)S(1)} %pad_maximum_fusion.3), channel_id=2, replica_groups=mesh['img'=16,'proto'=32] {'proto'}, dimensions={0}, use_global_device_ids=true | all-gather | bytes 540672 | tf_op jit(solution)/shard_map/all_gather | solution.py:47
  156.2 15.0 %while.145 = (s32[]{:T(128)}, f32[8,512]{1,0:T(8,128)S(1)}, s32[]{:T(128)}, s32[6]{0:T(128)S(1)}, f32[6,512,512]{2,1,0:T(8,128)}, /*index=5*/s32[6]{0:T(128)S(1)...) while((s32[]{:T(128)}, f32[8,512]{1,0:T(8,128)S(1)}, ...), condition=%wide.region_13.14_spmd, body=%wide.region_11.13_spmd.sunk | while | flops 524299 | bytes 1067267 | solution.py:27
  162.0 1.4 fusion.77
  169.1 1.4 fusion.77
  171.3 15.0 %while.146 = (s32[]{:T(128)}, f32[8,512]{1,0:T(8,128)S(1)}, s32[]{:T(128)}, s32[6]{0:T(128)S(1)}, f32[6,512,512]{2,1,0:T(8,128)}, /*index=5*/s32[6]{0:T(128)S(1)...) while((s32[]{:T(128)}, f32[8,512]{1,0:T(8,128)S(1)}, ...), condition=%wide.region_16.17_spmd, body=%wide.region_14.16_spmd.sunk | while | flops 786443 | bytes 1073423 | solution.py:43
  176.9 1.5 fusion.78
  184.1 1.5 fusion.78
  186.3 64.8 %all-gather.1 = f32[32,8,512]{2,1,0:T(8,128)S(1)} all-gather(f32[2,8,512]{2,1,0:T(8,128)S(1)} %pad_maximum_fusion), channel_id=3, replica_groups=mesh['img'=16,'proto'=32] {'img'}, dimensions={0}, use_global_device_ids=true | all-gather | bytes 557056 | tf_op jit(solution)/shard_map/all_gather | solution.py:47
  251.3 13.8 %while.147 = (s32[]{:T(128)}, f32[4,512]{1,0:T(4,128)S(1)}, s32[]{:T(128)}, s32[6]{0:T(128)S(1)}, f32[6,512,512]{2,1,0:T(8,128)}, /*index=5*/s32[6]{0:T(128)S(1)...) while((s32[]{:T(128)}, f32[4,512]{1,0:T(4,128)S(1)}, ...), condition=%wide.region_21.22_spmd, body=%wide.region_19.21_spmd.sunk | while | flops 524299 | bytes 1067267 | solution.py:27
  256.4 1.4 fusion.79
  262.9 1.4 fusion.79
  265.0 15.3 %while.148 = (s32[]{:T(128)}, f32[4,512]{1,0:T(4,128)S(1)}, s32[]{:T(128)}, s32[6]{0:T(128)S(1)}, f32[6,512,512]{2,1,0:T(8,128)}, /*index=5*/s32[6]{0:T(128)S(1)...) while((s32[]{:T(128)}, f32[4,512]{1,0:T(4,128)S(1)}, ...), condition=%wide.region_24.25_spmd, body=%wide.region_22.24_spmd.sunk | while | flops 786443 | bytes 1073423 | solution.py:43
  270.8 1.5 fusion.80
  278.1 1.5 fusion.80
  280.4 103.7 %all-gather.2 = f32[64,4,512]{2,1,0:T(4,128)S(1)} all-gather(f32[2,4,512]{2,1,0:T(4,128)S(1)} %pad_maximum_fusion.4), channel_id=4, replica_groups=mesh['img'=16,'proto'=32] {'proto'}, dimensions={0}, use_global_device_ids=true | all-gather | bytes 540672 | tf_op jit(solution)/shard_map/all_gather | solution.py:47
  384.2 15.0 %while.149 = (s32[]{:T(128)}, f32[8,512]{1,0:T(8,128)S(1)}, s32[]{:T(128)}, s32[6]{0:T(128)S(1)}, f32[6,512,512]{2,1,0:T(8,128)}, /*index=5*/s32[6]{0:T(128)S(1)...) while((s32[]{:T(128)}, f32[8,512]{1,0:T(8,128)S(1)}, ...), condition=%wide.region_29.30_spmd, body=%wide.region_27.29_spmd.sunk | while | flops 524299 | bytes 1067267 | solution.py:27
  390.0 1.4 fusion.81
  397.1 1.4 fusion.81
  399.3 16.1 %while.150 = (s32[]{:T(128)}, f32[8,512]{1,0:T(8,128)S(1)}, s32[]{:T(128)}, s32[6]{0:T(128)S(1)}, f32[6,512,512]{2,1,0:T(8,128)}, /*index=5*/s32[6]{0:T(128)S(1)...) while((s32[]{:T(128)}, f32[8,512]{1,0:T(8,128)S(1)}, ...), condition=%wide.region_32.33_spmd, body=%wide.region_30.32_spmd.sunk | while | flops 786443 | bytes 1073423 | solution.py:43
  399.9 0.7 dynamic_slice.405
  402.7 0.7 dynamic_slice.406
  405.4 1.5 fusion.82
  407.7 0.7 dynamic_slice.405
  410.4 0.7 dynamic_slice.406
  413.2 1.5 fusion.82
  415.4 68.4 %all-gather.3 = f32[32,8,512]{2,1,0:T(8,128)S(1)} all-gather(f32[2,8,512]{2,1,0:T(8,128)S(1)} %pad_maximum_fusion.1), channel_id=5, replica_groups=mesh['img'=16,'proto'=32] {'img'}, dimensions={0}, use_global_device_ids=true | all-gather | bytes 557056 | tf_op jit(solution)/shard_map/all_gather | solution.py:47
  484.0 14.1 %while.151 = (s32[]{:T(128)}, f32[4,512]{1,0:T(4,128)S(1)}, s32[]{:T(128)}, s32[6]{0:T(128)S(1)}, f32[6,512,512]{2,1,0:T(8,128)}, /*index=5*/s32[6]{0:T(128)S(1)...) while((s32[]{:T(128)}, f32[4,512]{1,0:T(4,128)S(1)}, ...), condition=%wide.region_37.38_spmd, body=%wide.region_35.37_spmd.sunk | while | flops 524299 | bytes 1067267 | solution.py:27
  489.2 1.4 fusion.83
  495.9 1.4 fusion.83
  498.0 15.3 %while.152 = (s32[]{:T(128)}, f32[4,512]{1,0:T(4,128)S(1)}, s32[]{:T(128)}, s32[6]{0:T(128)S(1)}, f32[6,512,512]{2,1,0:T(8,128)}, /*index=5*/s32[6]{0:T(128)S(1)...) while((s32[]{:T(128)}, f32[4,512]{1,0:T(4,128)S(1)}, ...), condition=%wide.region_40.41_spmd, body=%wide.region_38.40_spmd.sunk | while | flops 786443 | bytes 1073423 | solution.py:43
  503.8 1.5 fusion.84
  511.1 1.5 fusion.84
  513.4 103.8 %all-gather.4 = f32[64,4,512]{2,1,0:T(4,128)S(1)} all-gather(f32[2,4,512]{2,1,0:T(4,128)S(1)} %pad_maximum_fusion.5), channel_id=6, replica_groups=mesh['img'=16,'proto'=32] {'proto'}, dimensions={0}, use_global_device_ids=true | all-gather | bytes 540672 | tf_op jit(solution)/shard_map/all_gather | solution.py:47
  617.4 15.2 %while.153 = (s32[]{:T(128)}, f32[8,512]{1,0:T(8,128)S(1)}, s32[]{:T(128)}, s32[6]{0:T(128)S(1)}, f32[6,512,512]{2,1,0:T(8,128)}, /*index=5*/s32[6]{0:T(128)S(1)...) while((s32[]{:T(128)}, f32[8,512]{1,0:T(8,128)S(1)}, ...), condition=%wide.region_45.46_spmd, body=%wide.region_43.45_spmd.sunk | while | flops 524299 | bytes 1067267 | solution.py:27
  623.2 1.4 fusion.85
  630.5 1.4 fusion.85
  632.6 15.3 %while.154 = (s32[]{:T(128)}, f32[8,512]{1,0:T(8,128)S(1)}, s32[]{:T(128)}, s32[6]{0:T(128)S(1)}, f32[6,512,512]{2,1,0:T(8,128)}, /*index=5*/s32[6]{0:T(128)S(1)...) while((s32[]{:T(128)}, f32[8,512]{1,0:T(8,128)S(1)}, ...), condition=%wide.region_48.49_spmd, body=%wide.region_46.48_spmd.sunk | while | flops 786443 | bytes 1073423 | solution.py:43
  638.4 1.5 fusion.86
  645.7 1.5 fusion.86
  647.9 71.2 %all-gather.5 = f32[32,8,512]{2,1,0:T(8,128)S(1)} all-gather(f32[2,8,512]{2,1,0:T(8,128)S(1)} %pad_maximum_fusion.2), channel_id=7, replica_groups=mesh['img'=16,'proto'=32] {'img'}, dimensions={0}, use_global_device_ids=true | all-gather | bytes 557056 | tf_op jit(solution)/shard_map/all_gather | solution.py:47
  719.2 2.4 broadcast_in_dim.37
  721.6 19.8 %while.155 = (s32[]{:T(128)}, f32[8,512,256]{2,1,0:T(8,128)}, s32[]{:T(128)}, s32[6]{0:T(128)S(1)}, f32[6,512,512]{2,1,0:T(8,128)}, /*index=5*/s32[6]{0:T(128)S(...) while((s32[]{:T(128)}, f32[8,512,256]{2,1,0:T(8,128)}, ...), condition=%wide.region_52.53_spmd, body=%wide.region_51.52_spmd.sunk | while | flops 135135248 | bytes 3420443 | solution.py:132
  724.9 1.1 constant_dynamic-slice_fusion.43
  728.7 2.5 fusion.89
  734.5 1.1 constant_dynamic-slice_fusion.43
  738.3 2.5 fusion.89
  741.4 3.8 convert_element_type.15
  745.8 124.9 %reduce-scatter.2.cloned.1.call-done = bf16[256,256]{1,0:T(8,128)(2,1)} async-done(((bf16[4096,256]{1,0:T(8,128)(2,1)}), bf16[256,256]{1,0:T(8,128)(2,1)}) %reduce-scatter.2.cloned.1.call-update) | async-done | bytes 131088 | tf_op jit(solution)/shard_map/reduce_scatter | solution.py:135
  870.7 1.6 convert_element_type.17
  (161 shorter events, 30.5 us)
Async XLA Ops:
  7.2 4.9 copy-start.2
  7.2 4.9 copy-start.1
  7.2 4.9 copy-start
  7.2 863.5 %reduce-scatter.2.cloned.1.call-start = ((), (), s32[]{:S(2)}) async-start(), calls=%async_computation.1 | async-start | bytes 2228224 | tf_op jit(solution)/shard_map/reduce_scatter | solution.py:135
Sparse Core Ops, SparseCore 0:
  745.4 125.3 reduce-scatter.1

commit v2 on v1

--- a/solution.py
+++ b/solution.py
@@ -1,8 +1,11 @@
+import functools
 import math
 
 import jax
 import jax.numpy as jnp
 from jax import lax
+from jax.experimental import pallas as pl
+from jax.experimental.pallas import tpu as pltpu
 from jax.sharding import PartitionSpec as P
 
 E = 256
@@ -43,8 +46,64 @@
     return lax.fori_loop(0, live_slots, advance, jnp.zeros_like(tops))
 
 
+def gather_kernel(axis, x_ref, out_ref, landed, send_sems, recv_sems):
+    count = lax.axis_size(axis)
+    me = lax.axis_index(axis)
+
+    def peer_copy(peer, slot):
+        return pltpu.make_async_remote_copy(
+            src_ref=x_ref,
+            dst_ref=landed.at[slot],
+            send_sem=send_sems.at[slot],
+            recv_sem=recv_sems.at[slot],
+            device_id={axis: peer},
+            device_id_type=pl.DeviceIdType.MESH,
+        )
+
+    landed[me] = x_ref[...]
+
+    def send(step, carry):
+        peer = lax.rem(me + step, count)
+        peer_copy(peer, me).start()
+        return carry
+
+    lax.fori_loop(1, count, send, 0)
+
+    def receive(step, carry):
+        peer = lax.rem(me + count - step, count)
+        peer_copy(peer, peer).wait_recv()
+        return carry
+
+    lax.fori_loop(1, count, receive, 0)
+
+    def drain(step, carry):
+        peer = lax.rem(me + step, count)
+        peer_copy(peer, me).wait_send()
+        return carry
+
+    lax.fori_loop(1, count, drain, 0)
+    out_ref[...] = landed[...]
+
+
+def gather_peers(block, axis):
+    count = lax.axis_size(axis)
+    shape = (count,) + block.shape
+    return pl.pallas_call(
+        functools.partial(gather_kernel, axis),
+        out_shape=jax.ShapeDtypeStruct(shape, block.dtype),
+        in_specs=[pl.BlockSpec(memory_space=pltpu.VMEM)],
+        out_specs=pl.BlockSpec(memory_space=pltpu.VMEM),
+        scratch_shapes=[
+            pltpu.VMEM(shape, block.dtype),
+            pltpu.SemaphoreType.DMA((count,)),
+            pltpu.SemaphoreType.DMA((count,)),
+        ],
+        compiler_params=pltpu.CompilerParams(has_side_effects=True),
+    )(block)
+
+
 def merge_tops(local_top, local_mass, axis):
-    gathered = lax.all_gather(jnp.stack([local_top, local_mass]), axis)
+    gathered = gather_peers(jnp.stack([local_top, local_mass]), axis)
     tops, masses = gathered[:, 0], gathered[:, 1]
     highest = jnp.max(tops, axis=0)
     summed = jnp.sum(masses * jnp.exp(tops - highest[None]), axis=0)

time: 890 us -> 910 us (1.022)
  blocking collectives: 519 us -> 0 us
  Pallas kernels: 0 us -> 463 us
  loops' own time: 126 us -> 190 us
  waiting for transfers between devices: 125 us -> 82.4 us
  other arithmetic: 42.6 us -> 75.6 us
  local copies, waits for them, and re-layouts: 42.6 us -> 58.4 us
    all_gather x6 -> x0, blocking collectives: 519 us -> none  [merge_tops(): gathered = lax.all_gather(jnp.stack([local_top, local_mass]), axis)]
    pallas_call x0 -> x6, Pallas kernels: none -> 463 us  [gather_peers(): pl.pallas_call(functools.partial(gather_kernel, axis), out_shape=jax.Shap...]
    reduce_scatter x1, waiting for transfers between devices: 125 us -> 82.4 us  [shards(): lax.psum_scatter(partial_value.reshape(PB_DEV * TILE, E).astype(jnp.bfloa...]
    another operation x6, loops' own time: 52.1 us -> 80.9 us  [running_top(): lax.fori_loop(0, live_slots, advance, jnp.full((block_count, TILE), far_b...]
    another operation x6, loops' own time: 54.6 us -> 80.9 us  [running_mass(): return lax.fori_loop(0, live_slots, advance, jnp.zeros_like(tops))]
    reduce_sum x12 -> x18, other arithmetic: 18.1 us -> 27.1 us  [advance(): jnp.sum(jnp.exp(values_of(position) - jnp.expand_dims(top_here, reduced))...]
    reduce_max x12 -> x18, other arithmetic: 16.5 us -> 24.8 us  [advance(): local_top = jnp.max(values_of(position), axis=reduced)]
    dynamic_slice x24 -> x36, local copies, waits for them, and re-layouts: 14.8 us -> 21.1 us  [advance(): target = slot_blocks[position]]
where the time goes in v2:
time: 910 us; the launch traced here: 898 us
  Pallas kernels  463 us (51%)
  loops' own time  190 us (21%)
  waiting for transfers between devices  82.4 us (9%)
  other arithmetic  75.6 us (8%)
  local copies, waits for them, and re-layouts  58.4 us (6%)
  matrix products  14.4 us (2%)
  between operations  14.3 us (2%)
    pallas_call x6, Pallas kernels, gather_peers(): pl.pallas_call(functools.partial(gather_kernel, axis), out_shape=jax.Shap...  463 us
    reduce_scatter x1, waiting for transfers between devices, shards(): lax.psum_scatter(partial_value.reshape(PB_DEV * TILE, E).astype(jnp.bfloa...  82.4 us
    another operation x6, loops' own time, running_mass(): return lax.fori_loop(0, live_slots, advance, jnp.zeros_like(tops))  80.9 us
    another operation x6, loops' own time, running_top(): lax.fori_loop(0, live_slots, advance, jnp.full((block_count, TILE), far_b...  80.9 us
    reduce_sum x18, other arithmetic, advance(): jnp.sum(jnp.exp(values_of(position) - jnp.expand_dims(top_here, reduced))...  27.1 us
    reduce_max x18, other arithmetic, advance(): local_top = jnp.max(values_of(position), axis=reduced)  24.8 us
    dynamic_slice x36, local copies, waits for them, and re-layouts, advance(): target = slot_blocks[position]  21.1 us
  transfers between devices with their start and end apart: 1, of which 1 were waited for; matrix products, arithmetic and copies ran while one was open for 0% of the time, Pallas kernels for 0%

profile of v2, /device:TPU:1, one launch (start us, length us, event | category | flops | bytes accessed | tf_op | source)
XLA Modules:
  0.0 898.2 jit_solution(2026430383290017743)
XLA Ops:
  7.2 1.4 reduce_sum.130
  8.7 3.5 broadcast_in_dim.38
  12.1 24.9 %while.142 = (s32[]{:T(128)}, f32[6,512,512]{2,1,0:T(8,128)}, s32[]{:T(128)}, s32[6]{0:T(128)S(1)}, bf16[4,512,256]{2,1,0:T(8,128)(2,1)S(1)}, /*index=5*/s32[6]{...) while((s32[]{:T(128)}, f32[6,512,512]{2,1,0:T(8,128)}, ...), condition=%wide.region_2.3_spmd, body=%wide.region_1.2_spmd.sunk | while | flops 134479888 | bytes 1573119 | solution.py:137
  17.9 2.3 fusion.75
  26.0 2.3 fusion.75
  34.1 2.3 fusion.75
  37.1 14.7 %while.143 = (s32[]{:T(128)}, f32[4,512]{1,0:T(4,128)S(1)}, s32[]{:T(128)}, s32[6]{0:T(128)S(1)}, f32[6,512,512]{2,1,0:T(8,128)}, /*index=5*/s32[]{:T(128)}, s32[]{:T(128)}, s32[]{:T(128)}, s32[]{:T(128)}) while((s32[]{:T(128)}, f32[4,512]{1,0:T(4,128)S(1)}, s32[]{:T(128)}, s32[6]{0:T(128)S(1)}, f32[6,512,512]{2,1,0:T(8,128)}, ...), condition=%wide.region_5.6_spmd, body=%wide.region_3.5_spmd.sunk | while | flops 262152 | bytes 1061049 | solution.py:30
  51.8 15.2 %while.144 = (s32[]{:T(128)}, f32[4,512]{1,0:T(4,128)S(1)}, s32[]{:T(128)}, s32[6]{0:T(128)S(1)}, f32[6,512,512]{2,1,0:T(8,128)}, /*index=5*/f32[4,512]{1,0:T(4,...) while((s32[]{:T(128)}, f32[4,512]{1,0:T(4,128)S(1)}, s32[]{:T(128)}, s32[6]{0:T(128)S(1)}, ...), condition=%wide.region_8.9_spmd, body=%wide.region_6.8_spmd.sunk | while | flops 524296 | bytes 1067205 | solution.py:46
  55.0 1.5 fusion.76
  59.9 1.5 fusion.76
  64.7 1.5 fusion.76
  67.6 89.4 %shard_map.68 = f32[32,2,4,512]{3,2,1,0:T(4,128)} custom-call(f32[2,4,512]{2,1,0:T(4,128)} %pad_maximum_fusion.3.x_ref), custom_call_target="tpu_custom_call" | custom-call | tf_op jit(solution)/shard_map/pallas_call | solution.py:91
  159.2 22.4 %while.145 = (s32[]{:T(128)}, f32[8,512]{1,0:T(8,128)S(1)}, s32[]{:T(128)}, s32[6]{0:T(128)S(1)}, f32[6,512,512]{2,1,0:T(8,128)}, /*index=5*/s32[6]{0:T(128)S(1)...) while((s32[]{:T(128)}, f32[8,512]{1,0:T(8,128)S(1)}, ...), condition=%wide.region_13.14_spmd, body=%wide.region_11.13_spmd.sunk | while | flops 524299 | bytes 1067267 | solution.py:30
  165.0 1.4 fusion.77
  172.2 1.4 fusion.77
  181.6 22.7 %while.146 = (s32[]{:T(128)}, f32[8,512]{1,0:T(8,128)S(1)}, s32[]{:T(128)}, s32[6]{0:T(128)S(1)}, f32[6,512,512]{2,1,0:T(8,128)}, /*index=5*/s32[6]{0:T(128)S(1)...) while((s32[]{:T(128)}, f32[8,512]{1,0:T(8,128)S(1)}, ...), condition=%wide.region_16.17_spmd, body=%wide.region_14.16_spmd.sunk | while | flops 786443 | bytes 1073423 | solution.py:46
  187.4 1.5 fusion.78
  194.7 1.5 fusion.78
  202.0 1.5 fusion.78
  204.9 77.0 %shard_map.69 = f32[16,2,8,512]{3,2,1,0:T(8,128)} custom-call(f32[2,8,512]{2,1,0:T(8,128)} %pad_maximum_fusion.x_ref), custom_call_target="tpu_custom_call" | custom-call | tf_op jit(solution)/shard_map/pallas_call | solution.py:91
  284.0 22.3 %while.147 = (s32[]{:T(128)}, f32[4,512]{1,0:T(4,128)S(1)}, s32[]{:T(128)}, s32[6]{0:T(128)S(1)}, f32[6,512,512]{2,1,0:T(8,128)}, /*index=5*/s32[6]{0:T(128)S(1)...) while((s32[]{:T(128)}, f32[4,512]{1,0:T(4,128)S(1)}, ...), condition=%wide.region_21.22_spmd, body=%wide.region_19.21_spmd.sunk | while | flops 524299 | bytes 1067267 | solution.py:30
  289.8 1.4 fusion.79
  297.0 1.4 fusion.79
  304.2 1.4 fusion.79
  306.3 22.8 %while.148 = (s32[]{:T(128)}, f32[4,512]{1,0:T(4,128)S(1)}, s32[]{:T(128)}, s32[6]{0:T(128)S(1)}, f32[6,512,512]{2,1,0:T(8,128)}, /*index=5*/s32[6]{0:T(128)S(1)...) while((s32[]{:T(128)}, f32[4,512]{1,0:T(4,128)S(1)}, ...), condition=%wide.region_24.25_spmd, body=%wide.region_22.24_spmd.sunk | while | flops 786443 | bytes 1073423 | solution.py:46
  312.1 1.5 fusion.80
  319.5 1.5 fusion.80
  326.9 1.5 fusion.80
  329.8 71.1 %shard_map.70 = f32[32,2,4,512]{3,2,1,0:T(4,128)} custom-call(f32[2,4,512]{2,1,0:T(4,128)} %pad_maximum_fusion.4.x_ref), custom_call_target="tpu_custom_call" | custom-call | tf_op jit(solution)/shard_map/pallas_call | solution.py:91
  403.1 22.4 %while.149 = (s32[]{:T(128)}, f32[8,512]{1,0:T(8,128)S(1)}, s32[]{:T(128)}, s32[6]{0:T(128)S(1)}, f32[6,512,512]{2,1,0:T(8,128)}, /*index=5*/s32[6]{0:T(128)S(1)...) while((s32[]{:T(128)}, f32[8,512]{1,0:T(8,128)S(1)}, ...), condition=%wide.region_29.30_spmd, body=%wide.region_27.29_spmd.sunk | while | flops 524299 | bytes 1067267 | solution.py:30
  408.9 1.4 fusion.81
  416.1 1.4 fusion.81
  423.3 1.4 fusion.81
  425.5 22.7 %while.150 = (s32[]{:T(128)}, f32[8,512]{1,0:T(8,128)S(1)}, s32[]{:T(128)}, s32[6]{0:T(128)S(1)}, f32[6,512,512]{2,1,0:T(8,128)}, /*index=5*/s32[6]{0:T(128)S(1)...) while((s32[]{:T(128)}, f32[8,512]{1,0:T(8,128)S(1)}, ...), condition=%wide.region_32.33_spmd, body=%wide.region_30.32_spmd.sunk | while | flops 786443 | bytes 1073423 | solution.py:46
  431.2 1.5 fusion.82
  438.6 1.5 fusion.82
  445.9 1.5 fusion.82
  448.8 77.0 %shard_map.71 = f32[16,2,8,512]{3,2,1,0:T(8,128)} custom-call(f32[2,8,512]{2,1,0:T(8,128)} %pad_maximum_fusion.1.x_ref), custom_call_target="tpu_custom_call" | custom-call | tf_op jit(solution)/shard_map/pallas_call | solution.py:91
  527.9 22.3 %while.151 = (s32[]{:T(128)}, f32[4,512]{1,0:T(4,128)S(1)}, s32[]{:T(128)}, s32[6]{0:T(128)S(1)}, f32[6,512,512]{2,1,0:T(8,128)}, /*index=5*/s32[6]{0:T(128)S(1)...) while((s32[]{:T(128)}, f32[4,512]{1,0:T(4,128)S(1)}, ...), condition=%wide.region_37.38_spmd, body=%wide.region_35.37_spmd.sunk | while | flops 524299 | bytes 1067267 | solution.py:30
  533.7 1.4 fusion.83
  540.9 1.4 fusion.83
  548.1 1.4 fusion.83
  550.2 22.8 %while.152 = (s32[]{:T(128)}, f32[4,512]{1,0:T(4,128)S(1)}, s32[]{:T(128)}, s32[6]{0:T(128)S(1)}, f32[6,512,512]{2,1,0:T(8,128)}, /*index=5*/s32[6]{0:T(128)S(1)...) while((s32[]{:T(128)}, f32[4,512]{1,0:T(4,128)S(1)}, ...), condition=%wide.region_40.41_spmd, body=%wide.region_38.40_spmd.sunk | while | flops 786443 | bytes 1073423 | solution.py:46
  556.0 1.5 fusion.84
  563.4 1.5 fusion.84
  570.8 1.5 fusion.84
  573.7 71.1 %shard_map.72 = f32[32,2,4,512]{3,2,1,0:T(4,128)} custom-call(f32[2,4,512]{2,1,0:T(4,128)} %pad_maximum_fusion.5.x_ref), custom_call_target="tpu_custom_call" | custom-call | tf_op jit(solution)/shard_map/pallas_call | solution.py:91
  647.0 22.4 %while.153 = (s32[]{:T(128)}, f32[8,512]{1,0:T(8,128)S(1)}, s32[]{:T(128)}, s32[6]{0:T(128)S(1)}, f32[6,512,512]{2,1,0:T(8,128)}, /*index=5*/s32[6]{0:T(128)S(1)...) while((s32[]{:T(128)}, f32[8,512]{1,0:T(8,128)S(1)}, ...), condition=%wide.region_45.46_spmd, body=%wide.region_43.45_spmd.sunk | while | flops 524299 | bytes 1067267 | solution.py:30
  652.8 1.4 fusion.85
  660.0 1.4 fusion.85
  667.2 1.4 fusion.85
  669.4 22.7 %while.154 = (s32[]{:T(128)}, f32[8,512]{1,0:T(8,128)S(1)}, s32[]{:T(128)}, s32[6]{0:T(128)S(1)}, f32[6,512,512]{2,1,0:T(8,128)}, /*index=5*/s32[6]{0:T(128)S(1)...) while((s32[]{:T(128)}, f32[8,512]{1,0:T(8,128)S(1)}, ...), condition=%wide.region_48.49_spmd, body=%wide.region_46.48_spmd.sunk | while | flops 786443 | bytes 1073423 | solution.py:46
  675.1 1.5 fusion.86
  682.5 1.5 fusion.86
  689.8 1.5 fusion.86
  692.7 77.0 %shard_map.73 = f32[16,2,8,512]{3,2,1,0:T(8,128)} custom-call(f32[2,8,512]{2,1,0:T(8,128)} %pad_maximum_fusion.2.x_ref), custom_call_target="tpu_custom_call" | custom-call | tf_op jit(solution)/shard_map/pallas_call | solution.py:91
  771.8 2.4 broadcast_in_dim.37
  774.2 28.8 %while.155 = (s32[]{:T(128)}, f32[8,512,256]{2,1,0:T(8,128)}, s32[]{:T(128)}, s32[6]{0:T(128)S(1)}, f32[6,512,512]{2,1,0:T(8,128)}, /*index=5*/s32[6]{0:T(128)S(...) while((s32[]{:T(128)}, f32[8,512,256]{2,1,0:T(8,128)}, ...), condition=%wide.region_52.53_spmd, body=%wide.region_51.52_spmd.sunk | while | flops 135135248 | bytes 3420443 | solution.py:191
  781.0 2.5 fusion.89
  790.4 2.5 fusion.89
  799.8 2.5 fusion.89
  802.9 3.8 convert_element_type.15
  807.3 82.4 %reduce-scatter.2.cloned.1.call-done = bf16[256,256]{1,0:T(8,128)(2,1)} async-done(((bf16[4096,256]{1,0:T(8,128)(2,1)}), bf16[256,256]{1,0:T(8,128)(2,1)}) %reduce-scatter.2.cloned.1.call-update) | async-done | bytes 131088 | tf_op jit(solution)/shard_map/reduce_scatter | solution.py:194
  889.8 1.6 convert_element_type.17
  (238 shorter events, 74.9 us)
Async XLA Ops:
  7.2 5.0 copy-start.2
  7.2 5.0 copy-start.1
  7.2 5.0 copy-start
  7.2 882.6 %reduce-scatter.2.cloned.1.call-start = ((), (), s32[]{:S(2)}) async-start(), calls=%async_computation.1 | async-start | bytes 2228224 | tf_op jit(solution)/shard_map/reduce_scatter | solution.py:194
Sparse Core Ops, SparseCore 0:
  806.9 82.8 reduce-scatter.1

commit v3 on v2

--- a/solution.py
+++ b/solution.py
@@ -110,86 +110,110 @@
     return highest, summed
 
 
+def slot_specs():
+    return [pl.BlockSpec(memory_space=pltpu.SMEM)] * 3
+
+
+def whole_specs(count):
+    return [pl.BlockSpec(memory_space=pltpu.VMEM)] * count
+
+
+def pass_kernel(along_rows, rows_ref, protos_ref, valid_ref, images_ref, prototypes_ref,
+                other_ref, top_ref, mass_ref):
+    top_ref[...] = jnp.full(top_ref.shape, far_below, jnp.float32)
+    mass_ref[...] = jnp.zeros(mass_ref.shape, jnp.float32)
+    score_scale = float(E) ** (-0.5)
+    for position in range(MAXT):
+
+        @pl.when(valid_ref[position] == 1)
+        def _():
+            row_block = rows_ref[position]
+            proto_block = protos_ref[position]
+            rows_here = images_ref[pl.ds(pl.multiple_of(row_block * TILE, TILE), TILE), :]
+            protos_here = prototypes_ref[pl.ds(pl.multiple_of(proto_block * TILE, TILE), TILE), :]
+            if along_rows:
+                first, second, other_block, target = protos_here, rows_here, proto_block, row_block
+            else:
+                first, second, other_block, target = rows_here, protos_here, row_block, proto_block
+            products = lax.dot_general(
+                first, second, (((1,), (1,)), ((), ())), preferred_element_type=jnp.float32
+            )
+            values = products * score_scale + other_ref[other_block]
+            local_top = jnp.max(values, axis=0, keepdims=True)
+            old_top = top_ref[target]
+            new_top = jnp.maximum(old_top, local_top)
+            local_mass = jnp.sum(jnp.exp(values - new_top), axis=0, keepdims=True)
+            mass_ref[target] = mass_ref[target] * jnp.exp(old_top - new_top) + local_mass
+            top_ref[target] = new_top
+
+
+def local_pass(along_rows, slots, images, prototypes, other_column):
+    blocks = RB_DEV if along_rows else PB_DEV
+    shape = jax.ShapeDtypeStruct((blocks, 1, TILE), jnp.float32)
+    return pl.pallas_call(
+        functools.partial(pass_kernel, along_rows),
+        out_shape=(shape, shape),
+        in_specs=slot_specs() + whole_specs(3),
+        out_specs=tuple(whole_specs(2)),
+    )(*slots, images, prototypes, other_column)
+
+
+def final_kernel(rows_ref, protos_ref, valid_ref, images_ref, prototypes_ref,
+                 col_ref, row_ref, out_ref):
+    out_ref[...] = jnp.zeros(out_ref.shape, jnp.float32)
+    score_scale = float(E) ** (-0.5)
+    for position in range(MAXT):
+
+        @pl.when(valid_ref[position] == 1)
+        def _():
+            row_block = rows_ref[position]
+            proto_block = protos_ref[position]
+            rows_here = images_ref[pl.ds(pl.multiple_of(row_block * TILE, TILE), TILE), :]
+            protos_here = prototypes_ref[pl.ds(pl.multiple_of(proto_block * TILE, TILE), TILE), :]
+            products = lax.dot_general(
+                protos_here, rows_here, (((1,), (1,)), ((), ())), preferred_element_type=jnp.float32
+            )
+            weights = jnp.exp(
+                products * score_scale + col_ref[proto_block] + row_ref[row_block]
+            ).astype(jnp.bfloat16)
+            out_ref[proto_block] += jnp.dot(weights, rows_here, preferred_element_type=jnp.float32)
+
+
+def final_pass(slots, images, prototypes, col_column, row_pot):
+    return pl.pallas_call(
+        final_kernel,
+        out_shape=jax.ShapeDtypeStruct((PB_DEV, TILE, E), jnp.float32),
+        in_specs=slot_specs() + whole_specs(4),
+        out_specs=pl.BlockSpec(memory_space=pltpu.VMEM),
+    )(*slots, images, prototypes, col_column, row_pot.reshape(RB_DEV, 1, TILE))
+
+
 def shards(images, prototypes, tile_row, tile_proto, tile_valid):
     img_count = lax.axis_size("img")
     proto_count = lax.axis_size("proto")
-    image_blocks = images.reshape(RB_DEV, TILE, E)
-    proto_blocks = prototypes.reshape(PB_DEV, TILE, E)
-    slot_rows = tile_row.reshape(MAXT)
-    slot_protos = tile_proto.reshape(MAXT)
-    live_slots = jnp.sum(tile_valid)
-    score_scale = float(E) ** (-0.5)
+    slots = (tile_row.reshape(MAXT), tile_proto.reshape(MAXT), tile_valid.reshape(MAXT))
     log_ratio = math.log(PB_DEV * proto_count / (RB_DEV * img_count))
-
-    def fresh_scores(position):
-        rows_here = lax.dynamic_index_in_dim(image_blocks, slot_rows[position], 0, keepdims=False)
-        protos_here = lax.dynamic_index_in_dim(
-            proto_blocks, slot_protos[position], 0, keepdims=False
-        )
-        products = lax.dot_general(
-            rows_here, protos_here, (((1,), (1,)), ((), ())), preferred_element_type=jnp.float32
-        )
-        return products * score_scale
-
-    def fill_cache(position, cache):
-        return lax.dynamic_update_index_in_dim(cache, fresh_scores(position), position, 0)
-
-    score_cache = lax.fori_loop(
-        0, live_slots, fill_cache, jnp.zeros((MAXT, TILE, TILE), jnp.float32)
-    )
-
-    def scores_at(position):
-        return lax.dynamic_index_in_dim(score_cache, position, 0, keepdims=False)
 
     col_pot = jnp.zeros((PB_DEV, TILE), jnp.float32)
     row_pot = jnp.zeros((RB_DEV, TILE), jnp.float32)
     for iteration in range(ITERS):
-
-        def row_values_of(position):
-            return scores_at(position) + lax.dynamic_index_in_dim(
-                col_pot, slot_protos[position], 0, keepdims=True
-            )
-
-        row_local_top = running_top(row_values_of, live_slots, 1, slot_rows, RB_DEV)
-        row_local_mass = running_mass(row_values_of, live_slots, 1, slot_rows, row_local_top)
-        row_highest, row_summed = merge_tops(row_local_top, row_local_mass, "proto")
+        row_local_top, row_local_mass = local_pass(
+            True, slots, images, prototypes, col_pot.reshape(PB_DEV, TILE, 1)
+        )
+        row_highest, row_summed = merge_tops(
+            row_local_top.reshape(RB_DEV, TILE), row_local_mass.reshape(RB_DEV, TILE), "proto"
+        )
         row_pot = log_ratio - (row_highest + jnp.log(row_summed))
-
-        def values_of(position):
-            return (
-                scores_at(position)
-                + lax.dynamic_index_in_dim(row_pot, slot_rows[position], 0, keepdims=False)[:, None]
-            )
-
-        local_top = running_top(values_of, live_slots, 0, slot_protos, PB_DEV)
-        local_mass = running_mass(values_of, live_slots, 0, slot_protos, local_top)
-        highest, summed = merge_tops(local_top, local_mass, "img")
+        local_top, local_mass = local_pass(
+            False, slots, images, prototypes, row_pot.reshape(RB_DEV, TILE, 1)
+        )
+        highest, summed = merge_tops(
+            local_top.reshape(PB_DEV, TILE), local_mass.reshape(PB_DEV, TILE), "img"
+        )
         col_pot = -(highest + jnp.log(summed))
 
-    def tile_term(position):
-        target = slot_protos[position]
-        source = slot_rows[position]
-        shifted = (
-            scores_at(position)
-            + lax.dynamic_index_in_dim(row_pot, source, 0, keepdims=False)[:, None]
-        )
-        weights = jnp.exp(
-            shifted + lax.dynamic_index_in_dim(col_pot, target, 0, keepdims=True)
-        ).astype(jnp.bfloat16)
-        rows_here = lax.dynamic_index_in_dim(image_blocks, source, 0, keepdims=False)
-        return lax.dot_general(
-            weights, rows_here, (((0,), (0,)), ((), ())), preferred_element_type=jnp.float32
-        )
-
-    def add_tile(position, partial_value):
-        target = slot_protos[position]
-        current = lax.dynamic_index_in_dim(partial_value, target, 0, keepdims=False)
-        return lax.dynamic_update_index_in_dim(
-            partial_value, current + tile_term(position), target, 0
-        )
-
-    partial_value = lax.fori_loop(
-        0, live_slots, add_tile, jnp.zeros((PB_DEV, TILE, E), jnp.float32)
+    partial_value = final_pass(
+        slots, images, prototypes, col_pot.reshape(PB_DEV, TILE, 1), row_pot
     )
     proto_share = lax.psum_scatter(
         partial_value.reshape(PB_DEV * TILE, E).astype(jnp.bfloat16),

time: 910 us -> 353 us (0.39)
  Pallas kernels: 463 us -> 237 us
  loops' own time: 190 us -> 0 us
  other arithmetic: 75.6 us -> 21.8 us
  local copies, waits for them, and re-layouts: 58.4 us -> 20.6 us
  waiting for transfers between devices: 82.4 us -> 55.4 us
  matrix products: 14.4 us -> 0 us
    pallas_call x6, Pallas kernels: 463 us -> 196 us  [gather_peers(): pl.pallas_call(functools.partial(gather_kernel, axis), out_shape=jax.Shap...]
    another operation x14 -> x0, loops' own time: 190 us -> none  [the longest x6 80.9 us: running_mass(): return lax.fori_loop(0, live_slots, advance, jnp.zeros_like(tops))]
    dynamic_slice x117 -> x0, local copies, waits for them, and re-layouts: 49.8 us -> none  [the longest x36 21.1 us: advance(): target = slot_blocks[position]]
    pallas_call x0 -> x7, Pallas kernels: none -> 41.4 us  [the longest x6 33.7 us: local_pass(): pl.pallas_call(functools.partial(pass_kernel, along_rows), out_shape=(sha...]
    reduce_sum x19 -> x0, other arithmetic: 28.6 us -> none  [the longest x18 27.1 us: advance(): jnp.sum(jnp.exp(values_of(position) - jnp.expand_dims(top_here, reduced))...]
    reduce_scatter x1, waiting for transfers between devices: 82.4 us -> 55.3 us  [shards(): lax.psum_scatter(partial_value.reshape(PB_DEV * TILE, E).astype(jnp.bfloa...]
    reduce_max x18 -> x0, other arithmetic: 24.8 us -> none  [advance(): local_top = jnp.max(values_of(position), axis=reduced)]
    dot_general x6 -> x0, matrix products: 14.4 us -> none  [the longest x3 7.51 us: tile_term(): lax.dot_general(weights, rows_here, (((0,), (0,)), ((), ())), preferred_e...]
where the time goes in v3:
time: 353 us; the launch traced here: 349 us
  Pallas kernels  237 us (67%)
  waiting for transfers between devices  55.4 us (16%)
  other arithmetic  21.8 us (6%)
  local copies, waits for them, and re-layouts  20.6 us (6%)
  between operations  14.1 us (4%)
    pallas_call x6, Pallas kernels, gather_peers(): pl.pallas_call(functools.partial(gather_kernel, axis), out_shape=jax.Shap...  196 us
    reduce_scatter x1, waiting for transfers between devices, shards(): lax.psum_scatter(partial_value.reshape(PB_DEV * TILE, E).astype(jnp.bfloa...  55.3 us
    pallas_call x6, Pallas kernels, local_pass(): pl.pallas_call(functools.partial(pass_kernel, along_rows), out_shape=(sha...  33.7 us
    unnamed x12, local copies, waits for them, and re-layouts  8.44 us
    pallas_call x1, Pallas kernels, final_pass(): pl.pallas_call(final_kernel, out_shape=jax.ShapeDtypeStruct((PB_DEV, TILE...  7.69 us
  transfers between devices with their start and end apart: 1, of which 1 were waited for; matrix products, arithmetic and copies ran while one was open for 0% of the time, Pallas kernels for 0%

profile of v3, /device:TPU:1, one launch (start us, length us, event | category | flops | bytes accessed | tf_op | source)
XLA Modules:
  0.0 349.3 jit_solution(17874213676860185180)
XLA Ops:
  7.2 0.0 reduce-scatter.2.cloned.1.call-start
  7.2 1.5 reshape.184.other_ref
  8.7 5.8 %shard_map.68 = (f32[4,1,512]{2,1,0:T(1,128)}, f32[4,1,512]{2,1,0:T(1,128)}) custom-call(s32[6]{0:T(128)} %bitcast.142, s32[6]{0:T(128)} %bitcast.149, s32[6]{0:T(128)} %bitcast.156, bf16[2048,256]{1,0:T(8,128)(2,1)} %images_ref.13, bf16[4096,256]{1,0:T(8,128)(2,1)} %prototypes_ref.13, f32[8,512,1]{2,1,0:T(8,128)} %reshape.184.other_ref), custom_call_target="tpu_custom_call" | custom-call | tf_op jit(solution)/shard_map/pallas_call | solution.py:153
  14.5 0.7 copy_bitcast_fusion.10
  15.2 0.6 pad_maximum_fusion.3.x_ref
  15.8 37.2 %shard_map.69 = f32[32,2,4,512]{3,2,1,0:T(4,128)} custom-call(f32[2,4,512]{2,1,0:T(4,128)} %pad_maximum_fusion.3.x_ref), custom_call_target="tpu_custom_call" | custom-call | tf_op jit(solution)/shard_map/pallas_call | solution.py:91
  53.1 1.0 bitcast_reduce_fusion.5
  54.1 1.2 fusion.17
  55.3 1.4 copy.17.other_ref
  56.6 5.4 %shard_map.70 = (f32[8,1,512]{2,1,0:T(1,128)}, f32[8,1,512]{2,1,0:T(1,128)}) custom-call(s32[6]{0:T(128)} %bitcast.143, s32[6]{0:T(128)} %bitcast.150, s32[6]{0:T(128)} %bitcast.157, bf16[2048,256]{1,0:T(8,128)(2,1)} %images_ref.13, bf16[4096,256]{1,0:T(8,128)(2,1)} %prototypes_ref.13, f32[4,512,1]{2,1,0:T(8,128)} %copy.17.other_ref), custom_call_target="tpu_custom_call" | custom-call | tf_op jit(solution)/shard_map/pallas_call | solution.py:153
  62.1 0.7 copy.64
  62.8 0.7 copy.63
  63.5 0.6 pad_maximum_fusion.x_ref
  64.1 34.0 %shard_map.71 = f32[16,2,8,512]{3,2,1,0:T(8,128)} custom-call(f32[2,8,512]{2,1,0:T(8,128)} %pad_maximum_fusion.x_ref), custom_call_target="tpu_custom_call" | custom-call | tf_op jit(solution)/shard_map/pallas_call | solution.py:91
  98.1 1.0 bitcast_reduce_fusion.4
  99.1 1.1 fusion.14
  100.2 2.0 copy.19.other_ref
  102.2 5.8 %shard_map.72 = (f32[4,1,512]{2,1,0:T(1,128)}, f32[4,1,512]{2,1,0:T(1,128)}) custom-call(s32[6]{0:T(128)} %bitcast.144, s32[6]{0:T(128)} %bitcast.151, s32[6]{0:T(128)} %bitcast.158, bf16[2048,256]{1,0:T(8,128)(2,1)} %images_ref.13, bf16[4096,256]{1,0:T(8,128)(2,1)} %prototypes_ref.13, f32[8,512,1]{2,1,0:T(8,128)} %copy.19.other_ref), custom_call_target="tpu_custom_call" | custom-call | tf_op jit(solution)/shard_map/pallas_call | solution.py:153
  108.0 0.7 copy.68
  108.7 0.7 copy.67
  109.4 0.6 pad_maximum_fusion.4.x_ref
  110.0 28.3 %shard_map.73 = f32[32,2,4,512]{3,2,1,0:T(4,128)} custom-call(f32[2,4,512]{2,1,0:T(4,128)} %pad_maximum_fusion.4.x_ref), custom_call_target="tpu_custom_call" | custom-call | tf_op jit(solution)/shard_map/pallas_call | solution.py:91
  138.3 1.0 bitcast_reduce_fusion.3
  139.3 1.2 fusion.11
  140.5 1.4 copy.21.other_ref
  141.9 5.6 %shard_map.74 = (f32[8,1,512]{2,1,0:T(1,128)}, f32[8,1,512]{2,1,0:T(1,128)}) custom-call(s32[6]{0:T(128)} %bitcast.145, s32[6]{0:T(128)} %bitcast.152, s32[6]{0:T(128)} %bitcast.159, bf16[2048,256]{1,0:T(8,128)(2,1)} %images_ref.13, bf16[4096,256]{1,0:T(8,128)(2,1)} %prototypes_ref.13, f32[4,512,1]{2,1,0:T(8,128)} %copy.21.other_ref), custom_call_target="tpu_custom_call" | custom-call | tf_op jit(solution)/shard_map/pallas_call | solution.py:153
  147.5 0.7 copy.62
  148.2 0.7 copy.61
  148.9 0.6 pad_maximum_fusion.1.x_ref
  149.5 34.0 %shard_map.75 = f32[16,2,8,512]{3,2,1,0:T(8,128)} custom-call(f32[2,8,512]{2,1,0:T(8,128)} %pad_maximum_fusion.1.x_ref), custom_call_target="tpu_custom_call" | custom-call | tf_op jit(solution)/shard_map/pallas_call | solution.py:91
  183.5 1.0 bitcast_reduce_fusion.2
  184.5 1.1 fusion.8
  185.6 2.0 copy.23.other_ref
  187.6 5.8 %shard_map.76 = (f32[4,1,512]{2,1,0:T(1,128)}, f32[4,1,512]{2,1,0:T(1,128)}) custom-call(s32[6]{0:T(128)} %bitcast.146, s32[6]{0:T(128)} %bitcast.153, s32[6]{0:T(128)} %bitcast.160, bf16[2048,256]{1,0:T(8,128)(2,1)} %images_ref.13, bf16[4096,256]{1,0:T(8,128)(2,1)} %prototypes_ref.13, f32[8,512,1]{2,1,0:T(8,128)} %copy.23.other_ref), custom_call_target="tpu_custom_call" | custom-call | tf_op jit(solution)/shard_map/pallas_call | solution.py:153
  193.4 0.7 copy.66
  194.1 0.7 copy.65
  194.8 0.6 pad_maximum_fusion.5.x_ref
  195.4 28.3 %shard_map.77 = f32[32,2,4,512]{3,2,1,0:T(4,128)} custom-call(f32[2,4,512]{2,1,0:T(4,128)} %pad_maximum_fusion.5.x_ref), custom_call_target="tpu_custom_call" | custom-call | tf_op jit(solution)/shard_map/pallas_call | solution.py:91
  223.7 1.0 bitcast_reduce_fusion.1
  224.7 1.2 fusion.5
  225.9 0.6 sub.115.row_ref
  226.5 1.4 copy.25.other_ref
  227.9 5.4 %shard_map.78 = (f32[8,1,512]{2,1,0:T(1,128)}, f32[8,1,512]{2,1,0:T(1,128)}) custom-call(s32[6]{0:T(128)} %bitcast.147, s32[6]{0:T(128)} %bitcast.154, s32[6]{0:T(128)} %bitcast.161, bf16[2048,256]{1,0:T(8,128)(2,1)} %images_ref.13, bf16[4096,256]{1,0:T(8,128)(2,1)} %prototypes_ref.13, f32[4,512,1]{2,1,0:T(8,128)} %copy.25.other_ref), custom_call_target="tpu_custom_call" | custom-call | tf_op jit(solution)/shard_map/pallas_call | solution.py:153
  233.3 0.7 copy.60
  234.0 0.7 copy.59
  234.7 0.6 pad_maximum_fusion.2.x_ref
  235.3 34.0 %shard_map.79 = f32[16,2,8,512]{3,2,1,0:T(8,128)} custom-call(f32[2,8,512]{2,1,0:T(8,128)} %pad_maximum_fusion.2.x_ref), custom_call_target="tpu_custom_call" | custom-call | tf_op jit(solution)/shard_map/pallas_call | solution.py:91
  269.4 1.0 bitcast_reduce_fusion
  270.3 1.1 fusion.2
  271.4 2.0 copy.27.col_ref
  273.4 7.7 %shard_map.80 = f32[8,512,256]{2,1,0:T(8,128)} custom-call(s32[6]{0:T(128)} %bitcast.148, s32[6]{0:T(128)} %bitcast.155, s32[6]{0:T(128)} %bitcast.162, bf16[2048,256]{1,0:T(8,128)(2,1)} %images_ref.13, bf16[4096,256]{1,0:T(8,128)(2,1)} %prototypes_ref.13, f32[8,512,1]{2,1,0:T(8,128)} %copy.27.col_ref, f32[4,1,512]{2,1,0:T(1,128)} %sub.115.row_ref), custom_call_target="tpu_custom_call" | custom-call | tf_op jit(solution)/shard_map/pallas_call | solution.py:183
  281.1 3.8 %convert_element_type.9 = bf16[8,512,256]{2,1,0:T(8,128)(2,1)} convert(f32[8,512,256]{2,1,0:T(8,128)} %shard_map.80) | non-fusion elementwise | flops 1048576 | bytes 6291456 | tf_op jit(solution)/shard_map/convert_element_type | solution.py:219
  284.9 0.0 reduce-scatter.2.cloned.1.call-update
  284.9 0.6 copy.46
  285.5 55.3 %reduce-scatter.2.cloned.1.call-done = bf16[256,256]{1,0:T(8,128)(2,1)} async-done(((bf16[4096,256]{1,0:T(8,128)(2,1)}), bf16[256,256]{1,0:T(8,128)(2,1)}) %reduce-scatter.2.cloned.1.call-update) | async-done | bytes 131088 | tf_op jit(solution)/shard_map/reduce_scatter | solution.py:218
  340.8 1.6 convert_element_type.11
  (6 shorter events, 0.1 us)
Async XLA Ops:
  7.2 333.7 %reduce-scatter.2.cloned.1.call-start = ((), (), s32[]{:S(2)}) async-start(), calls=%async_computation.1 | async-start | bytes 2228224 | tf_op jit(solution)/shard_map/reduce_scatter | solution.py:218
Sparse Core Ops, SparseCore 0:
  285.0 55.7 reduce-scatter.1

commit v4 on v3

--- a/solution.py
+++ b/solution.py
@@ -188,33 +188,178 @@
     )(*slots, images, prototypes, col_column, row_pot.reshape(RB_DEV, 1, TILE))
 
 
+def to_column(lanes):
+    padded = jnp.concatenate(
+        [lanes, jnp.zeros((8 - lanes.shape[0], TILE), jnp.float32)], axis=0
+    ) if lanes.shape[0] < 8 else lanes
+    return jnp.transpose(padded)
+
+
+def exchange(axis, count, stage, local, packed, landed, send_sems, recv_sems):
+    me = lax.axis_index(axis)
+    packed[...] = local
+    landed[stage, me] = local
+
+    def peer_copy(peer, slot):
+        return pltpu.make_async_remote_copy(
+            src_ref=packed,
+            dst_ref=landed.at[stage, slot],
+            send_sem=send_sems.at[stage, peer],
+            recv_sem=recv_sems.at[stage, slot],
+            device_id={axis: peer},
+            device_id_type=pl.DeviceIdType.MESH,
+        )
+
+    def send(step, carry):
+        peer = lax.rem(me + step, count)
+        peer_copy(peer, me).start()
+        return carry
+
+    lax.fori_loop(1, count, send, 0)
+
+    def receive(step, carry):
+        peer = lax.rem(me + count - step, count)
+        peer_copy(peer, peer).wait_recv()
+        return carry
+
+    lax.fori_loop(1, count, receive, 0)
+
+    def drain(step, carry):
+        peer = lax.rem(me + step, count)
+        peer_copy(peer, me).wait_send()
+        return carry
+
+    lax.fori_loop(1, count, drain, 0)
+    gathered = landed[stage]
+    tops, masses = gathered[:, 0], gathered[:, 1]
+    highest = jnp.max(tops, axis=0)
+    summed = jnp.sum(masses * jnp.exp(tops - highest[None]), axis=0)
+    return highest, summed
+
+
+def pick_column(columns, chosen_block, blocks):
+    picked = columns[:, 0:1]
+    for block in range(1, blocks):
+        picked = jnp.where(chosen_block == block, columns[:, block:block + 1], picked)
+    return picked
+
+
+def local_merge(along_rows, rows_ref, protos_ref, valid_ref, slot_images_ref, slot_protos_ref,
+                other_columns):
+    blocks = RB_DEV if along_rows else PB_DEV
+    other_blocks = PB_DEV if along_rows else RB_DEV
+    tops = [jnp.full((1, TILE), far_below, jnp.float32) for _ in range(blocks)]
+    masses = [jnp.zeros((1, TILE), jnp.float32) for _ in range(blocks)]
+    score_scale = float(E) ** (-0.5)
+    for position in range(MAXT):
+        row_block = rows_ref[position]
+        proto_block = protos_ref[position]
+        live = valid_ref[position] == 1
+        rows_here = slot_images_ref[position]
+        protos_here = slot_protos_ref[position]
+        if along_rows:
+            first, second, other_block, target = protos_here, rows_here, proto_block, row_block
+        else:
+            first, second, other_block, target = rows_here, protos_here, row_block, proto_block
+        products = lax.dot_general(
+            first, second, (((1,), (1,)), ((), ())), preferred_element_type=jnp.float32
+        )
+        values = products * score_scale + pick_column(other_columns, other_block, other_blocks)
+        local_top = jnp.max(values, axis=0, keepdims=True)
+        local_mass = jnp.sum(jnp.exp(values - local_top), axis=0, keepdims=True)
+        for block in range(blocks):
+            chosen = jnp.logical_and(live, target == block)
+            new_top = jnp.maximum(tops[block], local_top)
+            new_mass = masses[block] * jnp.exp(tops[block] - new_top) + local_mass * jnp.exp(
+                local_top - new_top
+            )
+            tops[block] = jnp.where(chosen, new_top, tops[block])
+            masses[block] = jnp.where(chosen, new_mass, masses[block])
+    return jnp.stack([jnp.concatenate(tops, axis=0), jnp.concatenate(masses, axis=0)])
+
+
+def sinkhorn_kernel(log_ratio, rows_ref, protos_ref, valid_ref, images_ref, prototypes_ref,
+                    row_out, col_out, col_columns_out,
+                    row_packed, col_packed, row_landed, col_landed,
+                    row_send, row_recv, col_send, col_recv):
+    proto_count = lax.axis_size("proto")
+    img_count = lax.axis_size("img")
+    proto_me = lax.axis_index("proto")
+    img_me = lax.axis_index("img")
+    barrier = pltpu.get_barrier_semaphore()
+
+    def greet_proto(step, carry):
+        peer = lax.rem(proto_me + step, proto_count)
+        pl.semaphore_signal(barrier, inc=1, device_id={"proto": peer},
+                            device_id_type=pl.DeviceIdType.MESH)
+        return carry
+
+    def greet_img(step, carry):
+        peer = lax.rem(img_me + step, img_count)
+        pl.semaphore_signal(barrier, inc=1, device_id={"img": peer},
+                            device_id_type=pl.DeviceIdType.MESH)
+        return carry
+
+    lax.fori_loop(1, proto_count, greet_proto, 0)
+    lax.fori_loop(1, img_count, greet_img, 0)
+    pl.semaphore_wait(barrier, proto_count + img_count - 2)
+
+    col_t = jnp.zeros((TILE, PB_DEV), jnp.float32)
+    for iteration in range(ITERS):
+        local = local_merge(True, rows_ref, protos_ref, valid_ref, images_ref, prototypes_ref,
+                            col_t)
+        highest, summed = exchange("proto", proto_count, iteration, local, row_packed,
+                                   row_landed, row_send, row_recv)
+        row_pot = log_ratio - (highest + jnp.log(summed))
+        row_t = to_column(row_pot)
+        local = local_merge(False, rows_ref, protos_ref, valid_ref, images_ref, prototypes_ref,
+                            row_t)
+        highest, summed = exchange("img", img_count, iteration, local, col_packed,
+                                   col_landed, col_send, col_recv)
+        col_pot = -(highest + jnp.log(summed))
+        col_t = to_column(col_pot)
+    row_out[...] = row_pot
+    col_out[...] = col_pot
+    for block in range(PB_DEV):
+        col_columns_out[block] = col_t[:, block:block + 1]
+
+
+def sinkhorn(slots, slot_images, slot_protos, log_ratio):
+    proto_count = lax.axis_size("proto")
+    img_count = lax.axis_size("img")
+    vmem = pltpu.VMEM
+    return pl.pallas_call(
+        functools.partial(sinkhorn_kernel, log_ratio),
+        out_shape=(
+            jax.ShapeDtypeStruct((RB_DEV, TILE), jnp.float32),
+            jax.ShapeDtypeStruct((PB_DEV, TILE), jnp.float32),
+            jax.ShapeDtypeStruct((PB_DEV, TILE, 1), jnp.float32),
+        ),
+        in_specs=slot_specs() + whole_specs(2),
+        out_specs=tuple(whole_specs(3)),
+        scratch_shapes=[
+            vmem((2, RB_DEV, TILE), jnp.float32),
+            vmem((2, PB_DEV, TILE), jnp.float32),
+            vmem((ITERS, proto_count, 2, RB_DEV, TILE), jnp.float32),
+            vmem((ITERS, img_count, 2, PB_DEV, TILE), jnp.float32),
+            pltpu.SemaphoreType.DMA((ITERS, proto_count)),
+            pltpu.SemaphoreType.DMA((ITERS, proto_count)),
+            pltpu.SemaphoreType.DMA((ITERS, img_count)),
+            pltpu.SemaphoreType.DMA((ITERS, img_count)),
+        ],
+        compiler_params=pltpu.CompilerParams(collective_id=0, has_side_effects=True),
+    )(*slots, slot_images, slot_protos)
+
+
 def shards(images, prototypes, tile_row, tile_proto, tile_valid):
     img_count = lax.axis_size("img")
     proto_count = lax.axis_size("proto")
     slots = (tile_row.reshape(MAXT), tile_proto.reshape(MAXT), tile_valid.reshape(MAXT))
     log_ratio = math.log(PB_DEV * proto_count / (RB_DEV * img_count))
-
-    col_pot = jnp.zeros((PB_DEV, TILE), jnp.float32)
-    row_pot = jnp.zeros((RB_DEV, TILE), jnp.float32)
-    for iteration in range(ITERS):
-        row_local_top, row_local_mass = local_pass(
-            True, slots, images, prototypes, col_pot.reshape(PB_DEV, TILE, 1)
-        )
-        row_highest, row_summed = merge_tops(
-            row_local_top.reshape(RB_DEV, TILE), row_local_mass.reshape(RB_DEV, TILE), "proto"
-        )
-        row_pot = log_ratio - (row_highest + jnp.log(row_summed))
-        local_top, local_mass = local_pass(
-            False, slots, images, prototypes, row_pot.reshape(RB_DEV, TILE, 1)
-        )
-        highest, summed = merge_tops(
-            local_top.reshape(PB_DEV, TILE), local_mass.reshape(PB_DEV, TILE), "img"
-        )
-        col_pot = -(highest + jnp.log(summed))
-
-    partial_value = final_pass(
-        slots, images, prototypes, col_pot.reshape(PB_DEV, TILE, 1), row_pot
-    )
+    slot_images = images.reshape(RB_DEV, TILE, E)[slots[0]]
+    slot_protos = prototypes.reshape(PB_DEV, TILE, E)[slots[1]]
+    row_pot, col_pot, col_columns = sinkhorn(slots, slot_images, slot_protos, log_ratio)
+    partial_value = final_pass(slots, images, prototypes, col_columns, row_pot)
     proto_share = lax.psum_scatter(
         partial_value.reshape(PB_DEV * TILE, E).astype(jnp.bfloat16),
         "img",

time: 353 us -> 222 us (0.63)
  Pallas kernels: 237 us -> 134 us
  other arithmetic: 21.8 us -> 6.69 us
  local copies, waits for them, and re-layouts: 20.6 us -> 7.7 us
    pallas_call x12 -> x1, Pallas kernels: 230 us -> 128 us  [sinkhorn(): pl.pallas_call(functools.partial(sinkhorn_kernel, log_ratio), out_shape=(...]
    unnamed x12 -> x5, local copies, waits for them, and re-layouts: 8.44 us -> 1.31 us
    reduce_sum x6 -> x0, other arithmetic: 6.72 us -> none  [merge_tops(): summed = jnp.sum(masses * jnp.exp(tops - highest[None]), axis=0)]
    reduce_max x6 -> x0, other arithmetic: 5.99 us -> none  [merge_tops(): highest = jnp.max(tops, axis=0)]
    neg x3 -> x0, local copies, waits for them, and re-layouts: 5.98 us -> none  [shards(): col_pot = -(highest + jnp.log(summed))]
    gather x0 -> x2, local copies, waits for them, and re-layouts: none -> 5.09 us  [the longest x1 3.24 us: shards(): slot_images = images.reshape(RB_DEV, TILE, E)[slots[0]]]
    sub x4 -> x0, local copies, waits for them, and re-layouts: 4.71 us -> none  [shards(): row_pot = log_ratio - (row_highest + jnp.log(row_summed))]
    another operation x6 -> x0, other arithmetic: 3.69 us -> none  [merge_tops(): gathered = gather_peers(jnp.stack([local_top, local_mass]), axis)]
where the time goes in v4:
time: 222 us; the launch traced here: 220 us
  Pallas kernels  134 us (60%)
  waiting for transfers between devices  57.3 us (26%)
  between operations  14.1 us (6%)
  local copies, waits for them, and re-layouts  7.7 us (3%)
  other arithmetic  6.69 us (3%)
    pallas_call x1, Pallas kernels, sinkhorn(): pl.pallas_call(functools.partial(sinkhorn_kernel, log_ratio), out_shape=(...  128 us
    reduce_scatter x1, waiting for transfers between devices, shards(): lax.psum_scatter(partial_value.reshape(PB_DEV * TILE, E).astype(jnp.bfloa...  57.2 us
    pallas_call x1, Pallas kernels, final_pass(): pl.pallas_call(final_kernel, out_shape=jax.ShapeDtypeStruct((PB_DEV, TILE...  5.61 us
  transfers between devices with their start and end apart: 1, of which 1 were waited for; matrix products, arithmetic and copies ran while one was open for 0% of the time, Pallas kernels for 0%

profile of v4, /device:TPU:1, one launch (start us, length us, event | category | flops | bytes accessed | tf_op | source)
XLA Modules:
  0.0 219.8 jit_solution(15757436809561740358)
XLA Ops:
  7.2 0.0 reduce-scatter.2.cloned.1.call-start
  7.2 0.7 fusion
  7.9 0.7 fusion.1
  8.5 0.0 copy-start
  8.6 3.2 %gather_fusion = bf16[6,512,256]{2,1,0:T(8,128)(2,1)} fusion(bf16[4,512,256]{2,1,0:T(8,128)(2,1)} %bitcast.17, s32[1024]{0:T(1024)S(1)} %pad_clamp_fusion.1), kind=kCustom, calls=%fused_computation | custom fusion | bytes 3145752 | tf_op jit(solution)/shard_map/gather | solution.py:359
  11.8 0.0 copy-done
  11.8 1.9 gather_fusion.1
  13.7 128.5 %shard_map.68 = (f32[4,512]{1,0:T(4,128)}, f32[8,512]{1,0:T(8,128)}, f32[8,512,1]{2,1,0:T(8,128)}) custom-call(s32[6]{0:T(128)} %bitcast.21, s32[6]{0:T(128)} %bitcast.23, s32[6]{0:T(128)} %bitcast.25, bf16[6,512,256]{2,1,0:T(8,128)(2,1)} %gather_fusion, bf16[6,512,256]{2,1,0:T(8,128)(2,1)} %gather_fusion.1), custom_call_target="tpu_custom_call" | custom-call | tf_op jit(solution)/shard_map/pallas_call | solution.py:331
  142.1 1.3 reshape.94.row_ref
  143.4 5.6 %shard_map.69 = f32[8,512,256]{2,1,0:T(8,128)} custom-call(s32[6]{0:T(128)} %bitcast.22, s32[6]{0:T(128)} %bitcast.24, s32[6]{0:T(128)} %bitcast.26, bf16[2048,256]{1,0:T(8,128)(2,1)} %images_ref.1, bf16[4096,256]{1,0:T(8,128)(2,1)} %prototypes_ref.1, f32[8,512,1]{2,1,0:T(8,128)} %get-tuple-element.5.col_ref, f32[4,1,512]{2,1,0:T(1,128)} %reshape.94.row_ref), custom_call_target="tpu_custom_call" | custom-call | tf_op jit(solution)/shard_map/pallas_call | solution.py:183
  149.1 3.7 %convert_element_type.9 = bf16[8,512,256]{2,1,0:T(8,128)(2,1)} convert(f32[8,512,256]{2,1,0:T(8,128)} %shard_map.69) | non-fusion elementwise | flops 1048576 | bytes 6291456 | tf_op jit(solution)/shard_map/convert_element_type | solution.py:364
  152.8 0.0 copy-start.1
  152.8 0.0 reduce-scatter.2.cloned.1.call-update
  152.8 0.7 copy-done.1
  153.5 0.6 copy.7
  154.1 57.2 %reduce-scatter.2.cloned.1.call-done = bf16[256,256]{1,0:T(8,128)(2,1)} async-done(((bf16[4096,256]{1,0:T(8,128)(2,1)}), bf16[256,256]{1,0:T(8,128)(2,1)}) %reduce-scatter.2.cloned.1.call-update) | async-done | bytes 131088 | tf_op jit(solution)/shard_map/reduce_scatter | solution.py:363
  211.4 1.6 convert_element_type.11
  (2 shorter events, 0.0 us)
Async XLA Ops:
  7.2 204.2 %reduce-scatter.2.cloned.1.call-start = ((), (), s32[]{:S(2)}) async-start(), calls=%async_computation.1 | async-start | bytes 2228224 | tf_op jit(solution)/shard_map/reduce_scatter | solution.py:363
  8.5 3.3 %copy-start = (bf16[4096,256]{1,0:T(8,128)(2,1)S(1)}, bf16[4096,256]{1,0:T(8,128)(2,1)}, u32[]{:S(2)}) copy-start(bf16[4096,256]{1,0:T(8,128)(2,1)} %prototypes_ref.1) | copy-start | bytes 6291460
  152.8 0.7 copy-start.1
Sparse Core Ops, SparseCore 0:
  152.9 58.3 reduce-scatter.1

commit v5 on v4

--- a/solution.py
+++ b/solution.py
@@ -231,9 +231,8 @@
 
     lax.fori_loop(1, count, drain, 0)
     gathered = landed[stage]
-    tops, masses = gathered[:, 0], gathered[:, 1]
-    highest = jnp.max(tops, axis=0)
-    summed = jnp.sum(masses * jnp.exp(tops - highest[None]), axis=0)
+    highest = jnp.max(gathered, axis=0)
+    summed = jnp.sum(jnp.exp(gathered - highest[None]), axis=0)
     return highest, summed
 
 
@@ -275,7 +274,7 @@
             )
             tops[block] = jnp.where(chosen, new_top, tops[block])
             masses[block] = jnp.where(chosen, new_mass, masses[block])
-    return jnp.stack([jnp.concatenate(tops, axis=0), jnp.concatenate(masses, axis=0)])
+    return jnp.concatenate(tops, axis=0) + jnp.log(jnp.concatenate(masses, axis=0))
 
 
 def sinkhorn_kernel(log_ratio, rows_ref, protos_ref, valid_ref, images_ref, prototypes_ref,
@@ -338,10 +337,10 @@
         in_specs=slot_specs() + whole_specs(2),
         out_specs=tuple(whole_specs(3)),
         scratch_shapes=[
-            vmem((2, RB_DEV, TILE), jnp.float32),
-            vmem((2, PB_DEV, TILE), jnp.float32),
-            vmem((ITERS, proto_count, 2, RB_DEV, TILE), jnp.float32),
-            vmem((ITERS, img_count, 2, PB_DEV, TILE), jnp.float32),
+            vmem((RB_DEV, TILE), jnp.float32),
+            vmem((PB_DEV, TILE), jnp.float32),
+            vmem((ITERS, proto_count, RB_DEV, TILE), jnp.float32),
+            vmem((ITERS, img_count, PB_DEV, TILE), jnp.float32),
             pltpu.SemaphoreType.DMA((ITERS, proto_count)),
             pltpu.SemaphoreType.DMA((ITERS, proto_count)),
             pltpu.SemaphoreType.DMA((ITERS, img_count)),

time: 222 us -> 190 us (0.86)
  Pallas kernels: 134 us -> 101 us
    pallas_call x1, Pallas kernels: 128 us -> 95.3 us  [sinkhorn(): pl.pallas_call(functools.partial(sinkhorn_kernel, log_ratio), out_shape=(...]
where the time goes in v5:
time: 190 us; the launch traced here: 188 us
  Pallas kernels  101 us (53%)
  waiting for transfers between devices  58.8 us (31%)
  between operations  14.1 us (7%)
  local copies, waits for them, and re-layouts  7.7 us (4%)
  other arithmetic  6.69 us (4%)
    pallas_call x1, Pallas kernels, sinkhorn(): pl.pallas_call(functools.partial(sinkhorn_kernel, log_ratio), out_shape=(...  95.3 us
    reduce_scatter x1, waiting for transfers between devices, shards(): lax.psum_scatter(partial_value.reshape(PB_DEV * TILE, E).astype(jnp.bfloa...  58.7 us
    pallas_call x1, Pallas kernels, final_pass(): pl.pallas_call(final_kernel, out_shape=jax.ShapeDtypeStruct((PB_DEV, TILE...  5.39 us
  transfers between devices with their start and end apart: 1, of which 1 were waited for; matrix products, arithmetic and copies ran while one was open for 0% of the time, Pallas kernels for 0%

profile of v5, /device:TPU:1, one launch (start us, length us, event | category | flops | bytes accessed | tf_op | source)
XLA Modules:
  0.0 187.9 jit_solution(12372170556329814112)
XLA Ops:
  7.2 0.0 reduce-scatter.2.cloned.1.call-start
  7.2 0.7 fusion
  7.9 0.7 fusion.1
  8.5 0.0 copy-start
  8.6 3.2 %gather_fusion = bf16[6,512,256]{2,1,0:T(8,128)(2,1)} fusion(bf16[4,512,256]{2,1,0:T(8,128)(2,1)} %bitcast.17, s32[1024]{0:T(1024)S(1)} %pad_clamp_fusion.1), kind=kCustom, calls=%fused_computation | custom fusion | bytes 3145752 | tf_op jit(solution)/shard_map/gather | solution.py:358
  11.8 0.0 copy-done
  11.8 1.9 gather_fusion.1
  13.7 95.3 %shard_map.68 = (f32[4,512]{1,0:T(4,128)}, f32[8,512]{1,0:T(8,128)}, f32[8,512,1]{2,1,0:T(8,128)}) custom-call(s32[6]{0:T(128)} %bitcast.21, s32[6]{0:T(128)} %bitcast.23, s32[6]{0:T(128)} %bitcast.25, bf16[6,512,256]{2,1,0:T(8,128)(2,1)} %gather_fusion, bf16[6,512,256]{2,1,0:T(8,128)(2,1)} %gather_fusion.1), custom_call_target="tpu_custom_call" | custom-call | tf_op jit(solution)/shard_map/pallas_call | solution.py:330
  108.9 1.3 reshape.94.row_ref
  110.2 5.4 %shard_map.69 = f32[8,512,256]{2,1,0:T(8,128)} custom-call(s32[6]{0:T(128)} %bitcast.22, s32[6]{0:T(128)} %bitcast.24, s32[6]{0:T(128)} %bitcast.26, bf16[2048,256]{1,0:T(8,128)(2,1)} %images_ref.1, bf16[4096,256]{1,0:T(8,128)(2,1)} %prototypes_ref.1, f32[8,512,1]{2,1,0:T(8,128)} %get-tuple-element.5.col_ref, f32[4,1,512]{2,1,0:T(1,128)} %reshape.94.row_ref), custom_call_target="tpu_custom_call" | custom-call | tf_op jit(solution)/shard_map/pallas_call | solution.py:183
  115.6 3.7 %convert_element_type.9 = bf16[8,512,256]{2,1,0:T(8,128)(2,1)} convert(f32[8,512,256]{2,1,0:T(8,128)} %shard_map.69) | non-fusion elementwise | flops 1048576 | bytes 6291456 | tf_op jit(solution)/shard_map/convert_element_type | solution.py:363
  119.4 0.0 copy-start.1
  119.4 0.0 reduce-scatter.2.cloned.1.call-update
  119.4 0.7 copy-done.1
  120.1 0.6 copy.7
  120.7 58.7 %reduce-scatter.2.cloned.1.call-done = bf16[256,256]{1,0:T(8,128)(2,1)} async-done(((bf16[4096,256]{1,0:T(8,128)(2,1)}), bf16[256,256]{1,0:T(8,128)(2,1)}) %reduce-scatter.2.cloned.1.call-update) | async-done | bytes 131088 | tf_op jit(solution)/shard_map/reduce_scatter | solution.py:362
  179.4 1.6 convert_element_type.11
  (2 shorter events, 0.0 us)
Async XLA Ops:
  7.2 172.3 %reduce-scatter.2.cloned.1.call-start = ((), (), s32[]{:S(2)}) async-start(), calls=%async_computation.1 | async-start | bytes 2228224 | tf_op jit(solution)/shard_map/reduce_scatter | solution.py:362
  8.5 3.3 %copy-start = (bf16[4096,256]{1,0:T(8,128)(2,1)S(1)}, bf16[4096,256]{1,0:T(8,128)(2,1)}, u32[]{:S(2)}) copy-start(bf16[4096,256]{1,0:T(8,128)(2,1)} %prototypes_ref.1) | copy-start | bytes 6291460
  119.4 0.7 copy-start.1
Sparse Core Ops, SparseCore 0:
  119.5 59.8 reduce-scatter.1

commit v6 on v5

--- a/solution.py
+++ b/solution.py
@@ -359,12 +359,14 @@
     slot_protos = prototypes.reshape(PB_DEV, TILE, E)[slots[1]]
     row_pot, col_pot, col_columns = sinkhorn(slots, slot_images, slot_protos, log_ratio)
     partial_value = final_pass(slots, images, prototypes, col_columns, row_pot)
-    proto_share = lax.psum_scatter(
-        partial_value.reshape(PB_DEV * TILE, E).astype(jnp.bfloat16),
+    img_count = lax.axis_size("img")
+    shares = lax.all_to_all(
+        partial_value.reshape(img_count, PB_DEV * TILE // img_count, E).astype(jnp.bfloat16),
         "img",
-        scatter_dimension=0,
-        tiled=True,
-    ).astype(jnp.float32)
+        0,
+        0,
+    )
+    proto_share = jnp.sum(shares.astype(jnp.float32), axis=0)
     return (proto_share, col_pot.reshape(PB_DEV * TILE))
 
 

time: 190 us -> 172 us (0.905)
  between operations: 14.1 us -> 0.66 us
  waiting for transfers between devices: 58.8 us -> 48.3 us
  starting transfers between devices: 0.04 us -> 8.3 us
    reduce_scatter x1 -> x0, waiting for transfers between devices: 58.7 us -> none  [shards(): lax.psum_scatter(partial_value.reshape(PB_DEV * TILE, E).astype(jnp.bfloa...]
    all_to_all x0 -> x1, waiting for transfers between devices: none -> 48.3 us  [shards(): lax.all_to_all(partial_value.reshape(img_count, PB_DEV * TILE // img_coun...]
    all_to_all x0 -> x1, starting transfers between devices: none -> 8.3 us  [shards(): lax.all_to_all(partial_value.reshape(img_count, PB_DEV * TILE // img_coun...]
    convert_element_type x2 -> x1, other arithmetic: 5.36 us -> 3.74 us  [shards(): partial_value.reshape(img_count, PB_DEV * TILE // img_count, E)]
where the time goes in v6:
time: 172 us
  Pallas kernels  101 us (59%)
  waiting for transfers between devices  48.3 us (28%)
  starting transfers between devices  8.3 us (5%)
  local copies, waits for them, and re-layouts  6.88 us (4%)
  other arithmetic  6.2 us (4%)
    pallas_call x1, Pallas kernels, sinkhorn(): pl.pallas_call(functools.partial(sinkhorn_kernel, log_ratio), out_shape=(...  95.6 us
    all_to_all x1, waiting for transfers between devices, shards(): lax.all_to_all(partial_value.reshape(img_count, PB_DEV * TILE // img_coun...  48.3 us
    all_to_all x1, starting transfers between devices, shards(): lax.all_to_all(partial_value.reshape(img_count, PB_DEV * TILE // img_coun...  8.3 us
    pallas_call x1, Pallas kernels, final_pass(): pl.pallas_call(final_kernel, out_shape=jax.ShapeDtypeStruct((PB_DEV, TILE...  5.6 us
    convert_element_type x1, other arithmetic, shards(): partial_value.reshape(img_count, PB_DEV * TILE // img_count, E)  3.74 us
  transfers between devices with their start and end apart: 1, of which 1 were waited for; matrix products, arithmetic and copies ran while one was open for 0% of the time, Pallas kernels for 0%

profile of v6, /device:TPU:1, one launch (start us, length us, event | category | flops | bytes accessed | tf_op | source)
XLA Modules:
  0.0 171.6 jit_solution(5188640575523093729)
XLA Ops:
  0.6 0.0 copy-start
  0.6 0.8 fusion
  1.4 0.7 fusion.1
  2.1 3.1 %gather_fusion = bf16[6,512,256]{2,1,0:T(8,128)(2,1)} fusion(bf16[4,512,256]{2,1,0:T(8,128)(2,1)} %bitcast.16, s32[1024]{0:T(1024)S(1)} %pad_clamp_fusion.1), kind=kCustom, calls=%fused_computation | custom fusion | bytes 3145752 | tf_op jit(solution)/shard_map/gather | solution.py:358
  5.2 0.0 copy-done
  5.2 1.9 %gather_fusion.1 = bf16[6,512,256]{2,1,0:T(8,128)(2,1)} fusion(bf16[8,512,256]{2,1,0:T(8,128)(2,1)S(1)} %bitcast.17, s32[1024]{0:T(1024)S(1)} %pad_clamp_fusion), kind=kCustom, calls=%fused_computation.1 | custom fusion | bytes 3145752 | tf_op jit(solution)/shard_map/gather | solution.py:359
  7.1 95.6 %shard_map.68 = (f32[4,512]{1,0:T(4,128)}, f32[8,512]{1,0:T(8,128)}, f32[8,512,1]{2,1,0:T(8,128)}) custom-call(s32[6]{0:T(128)} %bitcast.20, s32[6]{0:T(128)} %bitcast.22, s32[6]{0:T(128)} %bitcast.24, bf16[6,512,256]{2,1,0:T(8,128)(2,1)} %gather_fusion, bf16[6,512,256]{2,1,0:T(8,128)(2,1)} %gather_fusion.1), custom_call_target="tpu_custom_call" | custom-call | tf_op jit(solution)/shard_map/pallas_call | solution.py:330
  102.7 1.3 reshape.94.row_ref
  104.0 5.6 %shard_map.69 = f32[8,512,256]{2,1,0:T(8,128)} custom-call(s32[6]{0:T(128)} %bitcast.21, s32[6]{0:T(128)} %bitcast.23, s32[6]{0:T(128)} %bitcast.25, bf16[2048,256]{1,0:T(8,128)(2,1)} %images_ref.1, bf16[4096,256]{1,0:T(8,128)(2,1)} %prototypes_ref.1, f32[8,512,1]{2,1,0:T(8,128)} %get-tuple-element.5.col_ref, f32[4,1,512]{2,1,0:T(1,128)} %reshape.94.row_ref), custom_call_target="tpu_custom_call" | custom-call | tf_op jit(solution)/shard_map/pallas_call | solution.py:183
  109.6 3.7 %convert_element_type.9 = bf16[8,512,256]{2,1,0:T(8,128)(2,1)} convert(f32[8,512,256]{2,1,0:T(8,128)} %shard_map.69) | non-fusion elementwise | flops 1048576 | bytes 6291456 | tf_op jit(solution)/shard_map/convert_element_type | solution.py:364
  113.3 0.0 copy-start.1
  113.3 8.3 %all-to-all-start = ((bf16[16,256,256]{2,1,0:T(8,128)(2,1)}), bf16[16,256,256]{2,1,0:T(8,128)(2,1)S(1)}, u32[]{:S(2)}, u32[]{:S(2)}) async-start(bf16[16,256,256]{2,1,0:T(8,128)(2,1)} %bitcast.9), calls=%async_computation | async-start | bytes 4194304 | tf_op jit(solution)/shard_map/all_to_all | solution.py:363
  121.6 0.0 copy-done.1
  121.6 0.6 copy.7
  122.3 48.3 %all-to-all-done = bf16[16,256,256]{2,1,0:T(8,128)(2,1)S(1)} async-done(((bf16[16,256,256]{2,1,0:T(8,128)(2,1)}), bf16[16,256,256]{2,1,0:T(8,128)(2,1)S(1)}, u32[]{:S(2)}, u32[]{:S(2)}) %all-to-all-start) | async-done | bytes 2097184 | tf_op jit(solution)/shard_map/all_to_all | solution.py:363
  170.6 1.0 convert_reduce_fusion
  (2 shorter events, 0.0 us)
Async XLA Ops:
  0.6 4.6 %copy-start = (bf16[4096,256]{1,0:T(8,128)(2,1)S(1)}, bf16[4096,256]{1,0:T(8,128)(2,1)}, u32[]{:S(2)}) copy-start(bf16[4096,256]{1,0:T(8,128)(2,1)} %prototypes_ref.1) | copy-start | bytes 6291460
  113.3 8.3 %copy-start.1 = (f32[8,512]{1,0:T(8,128)S(1)}, f32[8,512]{1,0:T(8,128)}, u32[]{:S(2)}) copy-start(f32[8,512]{1,0:T(8,128)} %get-tuple-element.7) | copy-start | bytes 49156
  113.3 57.3 %all-to-all-start = ((bf16[16,256,256]{2,1,0:T(8,128)(2,1)}), bf16[16,256,256]{2,1,0:T(8,128)(2,1)S(1)}, u32[]{:S(2)}, u32[]{:S(2)}) async-start(bf16[16,256,256]{2,1,0:T(8,128)(2,1)} %bitcast.9), calls=%async_computation | async-start | bytes 4194304 | tf_op jit(solution)/shard_map/all_to_all | solution.py:363

commit v7 on v6

--- a/solution.py
+++ b/solution.py
@@ -195,45 +195,55 @@
     return jnp.transpose(padded)
 
 
-def exchange(axis, count, stage, local, packed, landed, send_sems, recv_sems):
+def stage_peer(axis, size, stride, step):
     me = lax.axis_index(axis)
+    place = lax.rem(me // stride, size)
+    return me + (lax.rem(place + step, size) - place) * stride, place
+
+
+def exchange_stage(axis, size, stride, stage, local, packed, landed, send_sems, recv_sems):
+    place = stage_peer(axis, size, stride, 0)[1]
     packed[...] = local
-    landed[stage, me] = local
-
-    def peer_copy(peer, slot):
+    landed[stage, place] = local
+
+    def peer_copy(step, slot):
         return pltpu.make_async_remote_copy(
             src_ref=packed,
             dst_ref=landed.at[stage, slot],
-            send_sem=send_sems.at[stage, peer],
+            send_sem=send_sems.at[stage, lax.rem(place + step, size)],
             recv_sem=recv_sems.at[stage, slot],
-            device_id={axis: peer},
+            device_id={axis: stage_peer(axis, size, stride, step)[0]},
             device_id_type=pl.DeviceIdType.MESH,
         )
 
     def send(step, carry):
-        peer = lax.rem(me + step, count)
-        peer_copy(peer, me).start()
-        return carry
-
-    lax.fori_loop(1, count, send, 0)
+        peer_copy(step, place).start()
+        return carry
+
+    lax.fori_loop(1, size, send, 0)
 
     def receive(step, carry):
-        peer = lax.rem(me + count - step, count)
-        peer_copy(peer, peer).wait_recv()
-        return carry
-
-    lax.fori_loop(1, count, receive, 0)
+        peer_copy(size - step, lax.rem(place + size - step, size)).wait_recv()
+        return carry
+
+    lax.fori_loop(1, size, receive, 0)
 
     def drain(step, carry):
-        peer = lax.rem(me + step, count)
-        peer_copy(peer, me).wait_send()
-        return carry
-
-    lax.fori_loop(1, count, drain, 0)
+        peer_copy(step, place).wait_send()
+        return carry
+
+    lax.fori_loop(1, size, drain, 0)
     gathered = landed[stage]
     highest = jnp.max(gathered, axis=0)
-    summed = jnp.sum(jnp.exp(gathered - highest[None]), axis=0)
-    return highest, summed
+    return highest + jnp.log(jnp.sum(jnp.exp(gathered - highest[None]), axis=0))
+
+
+def exchange(axis, groups, stage, local, packed, landed_refs, send_refs, recv_refs):
+    for (size, stride), landed, send_sems, recv_sems in zip(groups, landed_refs, send_refs,
+                                                           recv_refs):
+        local = exchange_stage(axis, size, stride, stage, local, packed, landed, send_sems,
+                               recv_sems)
+    return local
 
 
 def pick_column(columns, chosen_block, blocks):
@@ -274,48 +284,53 @@
             )
             tops[block] = jnp.where(chosen, new_top, tops[block])
             masses[block] = jnp.where(chosen, new_mass, masses[block])
-    return jnp.concatenate(tops, axis=0) + jnp.log(jnp.concatenate(masses, axis=0))
-
-
-def sinkhorn_kernel(log_ratio, rows_ref, protos_ref, valid_ref, images_ref, prototypes_ref,
-                    row_out, col_out, col_columns_out,
-                    row_packed, col_packed, row_landed, col_landed,
-                    row_send, row_recv, col_send, col_recv):
+    return jnp.maximum(
+        jnp.concatenate(tops, axis=0) + jnp.log(jnp.concatenate(masses, axis=0)), far_below
+    )
+
+
+def axis_groups():
     proto_count = lax.axis_size("proto")
     img_count = lax.axis_size("img")
-    proto_me = lax.axis_index("proto")
-    img_me = lax.axis_index("img")
+    return {
+        "proto": ((PB_DEV, 1), (proto_count // PB_DEV, PB_DEV)),
+        "img": ((2, 1), (img_count // 2, 2)),
+    }
+
+
+def sinkhorn_kernel(log_ratio, rows_ref, protos_ref, valid_ref, images_ref, prototypes_ref,
+                    row_out, col_out, col_columns_out, row_packed, col_packed, *stage_refs):
+    groups = axis_groups()
+    row_refs = stage_refs[0:6]
+    col_refs = stage_refs[6:12]
     barrier = pltpu.get_barrier_semaphore()
-
-    def greet_proto(step, carry):
-        peer = lax.rem(proto_me + step, proto_count)
-        pl.semaphore_signal(barrier, inc=1, device_id={"proto": peer},
-                            device_id_type=pl.DeviceIdType.MESH)
-        return carry
-
-    def greet_img(step, carry):
-        peer = lax.rem(img_me + step, img_count)
-        pl.semaphore_signal(barrier, inc=1, device_id={"img": peer},
-                            device_id_type=pl.DeviceIdType.MESH)
-        return carry
-
-    lax.fori_loop(1, proto_count, greet_proto, 0)
-    lax.fori_loop(1, img_count, greet_img, 0)
-    pl.semaphore_wait(barrier, proto_count + img_count - 2)
+    greeted = 0
+    for axis in ("proto", "img"):
+        for size, stride in groups[axis]:
+
+            def greet(step, carry):
+                peer = stage_peer(axis, size, stride, step)[0]
+                pl.semaphore_signal(barrier, inc=1, device_id={axis: peer},
+                                    device_id_type=pl.DeviceIdType.MESH)
+                return carry
+
+            lax.fori_loop(1, size, greet, 0)
+            greeted += size - 1
+    pl.semaphore_wait(barrier, greeted)
 
     col_t = jnp.zeros((TILE, PB_DEV), jnp.float32)
     for iteration in range(ITERS):
         local = local_merge(True, rows_ref, protos_ref, valid_ref, images_ref, prototypes_ref,
                             col_t)
-        highest, summed = exchange("proto", proto_count, iteration, local, row_packed,
-                                   row_landed, row_send, row_recv)
-        row_pot = log_ratio - (highest + jnp.log(summed))
+        merged = exchange("proto", groups["proto"], iteration, local, row_packed,
+                          row_refs[0:2], row_refs[2:4], row_refs[4:6])
+        row_pot = log_ratio - merged
         row_t = to_column(row_pot)
         local = local_merge(False, rows_ref, protos_ref, valid_ref, images_ref, prototypes_ref,
                             row_t)
-        highest, summed = exchange("img", img_count, iteration, local, col_packed,
-                                   col_landed, col_send, col_recv)
-        col_pot = -(highest + jnp.log(summed))
+        merged = exchange("img", groups["img"], iteration, local, col_packed,
+                          col_refs[0:2], col_refs[2:4], col_refs[4:6])
+        col_pot = -merged
         col_t = to_column(col_pot)
     row_out[...] = row_pot
     col_out[...] = col_pot
@@ -324,9 +339,14 @@
 
 
 def sinkhorn(slots, slot_images, slot_protos, log_ratio):
-    proto_count = lax.axis_size("proto")
-    img_count = lax.axis_size("img")
+    groups = axis_groups()
     vmem = pltpu.VMEM
+    stage_scratch = []
+    for axis, blocks in (("proto", RB_DEV), ("img", PB_DEV)):
+        sizes = [size for size, _ in groups[axis]]
+        stage_scratch += [vmem((ITERS, size, blocks, TILE), jnp.float32) for size in sizes]
+        stage_scratch += [pltpu.SemaphoreType.DMA((ITERS, size)) for size in sizes]
+        stage_scratch += [pltpu.SemaphoreType.DMA((ITERS, size)) for size in sizes]
     return pl.pallas_call(
         functools.partial(sinkhorn_kernel, log_ratio),
         out_shape=(
@@ -339,13 +359,7 @@
         scratch_shapes=[
             vmem((RB_DEV, TILE), jnp.float32),
             vmem((PB_DEV, TILE), jnp.float32),
-            vmem((ITERS, proto_count, RB_DEV, TILE), jnp.float32),
-            vmem((ITERS, img_count, PB_DEV, TILE), jnp.float32),
-            pltpu.SemaphoreType.DMA((ITERS, proto_count)),
-            pltpu.SemaphoreType.DMA((ITERS, proto_count)),
-            pltpu.SemaphoreType.DMA((ITERS, img_count)),
-            pltpu.SemaphoreType.DMA((ITERS, img_count)),
-        ],
+        ] + stage_scratch,
         compiler_params=pltpu.CompilerParams(collective_id=0, has_side_effects=True),
     )(*slots, slot_images, slot_protos)
 

time: 172 us -> 165 us (0.959)
  Pallas kernels: 101 us -> 94.1 us
    pallas_call x1, Pallas kernels: 95.6 us -> 87.9 us  [sinkhorn(): pl.pallas_call(functools.partial(sinkhorn_kernel, log_ratio), out_shape=(...]
where the time goes in v7:
time: 165 us
  Pallas kernels  94.1 us (57%)
  waiting for transfers between devices  48.3 us (29%)
  starting transfers between devices  8.64 us (5%)
  local copies, waits for them, and re-layouts  6.88 us (4%)
  other arithmetic  6.2 us (4%)
    pallas_call x1, Pallas kernels, sinkhorn(): pl.pallas_call(functools.partial(sinkhorn_kernel, log_ratio), out_shape=(...  87.9 us
    all_to_all x1, waiting for transfers between devices, shards(): lax.all_to_all(partial_value.reshape(img_count, PB_DEV * TILE // img_coun...  48.3 us
    all_to_all x1, starting transfers between devices, shards(): lax.all_to_all(partial_value.reshape(img_count, PB_DEV * TILE // img_coun...  8.64 us
    pallas_call x1, Pallas kernels, final_pass(): pl.pallas_call(final_kernel, out_shape=jax.ShapeDtypeStruct((PB_DEV, TILE...  6.18 us
    convert_element_type x1, other arithmetic, shards(): partial_value.reshape(img_count, PB_DEV * TILE // img_count, E)  3.74 us
  transfers between devices with their start and end apart: 1, of which 1 were waited for; matrix products, arithmetic and copies ran while one was open for 0% of the time, Pallas kernels for 0%

profile of v7, /device:TPU:1, one launch (start us, length us, event | category | flops | bytes accessed | tf_op | source)
XLA Modules:
  0.0 164.8 jit_solution(10229970764345045064)
XLA Ops:
  0.6 0.0 copy-start
  0.6 0.8 fusion
  1.4 0.7 fusion.1
  2.1 3.1 %gather_fusion = bf16[6,512,256]{2,1,0:T(8,128)(2,1)} fusion(bf16[4,512,256]{2,1,0:T(8,128)(2,1)} %bitcast.16, s32[1024]{0:T(1024)S(1)} %pad_clamp_fusion.1), kind=kCustom, calls=%fused_computation | custom fusion | bytes 3145752 | tf_op jit(solution)/shard_map/gather | solution.py:372
  5.2 0.0 copy-done
  5.2 1.9 %gather_fusion.1 = bf16[6,512,256]{2,1,0:T(8,128)(2,1)} fusion(bf16[8,512,256]{2,1,0:T(8,128)(2,1)S(1)} %bitcast.17, s32[1024]{0:T(1024)S(1)} %pad_clamp_fusion), kind=kCustom, calls=%fused_computation.1 | custom fusion | bytes 3145752 | tf_op jit(solution)/shard_map/gather | solution.py:373
  7.1 87.9 %shard_map.68 = (f32[4,512]{1,0:T(4,128)}, f32[8,512]{1,0:T(8,128)}, f32[8,512,1]{2,1,0:T(8,128)}) custom-call(s32[6]{0:T(128)} %bitcast.20, s32[6]{0:T(128)} %bitcast.22, s32[6]{0:T(128)} %bitcast.24, bf16[6,512,256]{2,1,0:T(8,128)(2,1)} %gather_fusion, bf16[6,512,256]{2,1,0:T(8,128)(2,1)} %gather_fusion.1), custom_call_target="tpu_custom_call" | custom-call | tf_op jit(solution)/shard_map/pallas_call | solution.py:350
  95.0 1.3 reshape.94.row_ref
  96.3 6.2 %shard_map.69 = f32[8,512,256]{2,1,0:T(8,128)} custom-call(s32[6]{0:T(128)} %bitcast.21, s32[6]{0:T(128)} %bitcast.23, s32[6]{0:T(128)} %bitcast.25, bf16[2048,256]{1,0:T(8,128)(2,1)} %images_ref.1, bf16[4096,256]{1,0:T(8,128)(2,1)} %prototypes_ref.1, f32[8,512,1]{2,1,0:T(8,128)} %get-tuple-element.5.col_ref, f32[4,1,512]{2,1,0:T(1,128)} %reshape.94.row_ref), custom_call_target="tpu_custom_call" | custom-call | tf_op jit(solution)/shard_map/pallas_call | solution.py:183
  102.5 3.7 %convert_element_type.9 = bf16[8,512,256]{2,1,0:T(8,128)(2,1)} convert(f32[8,512,256]{2,1,0:T(8,128)} %shard_map.69) | non-fusion elementwise | flops 1048576 | bytes 6291456 | tf_op jit(solution)/shard_map/convert_element_type | solution.py:378
  106.2 0.0 copy-start.1
  106.2 8.6 %all-to-all-start = ((bf16[16,256,256]{2,1,0:T(8,128)(2,1)}), bf16[16,256,256]{2,1,0:T(8,128)(2,1)S(1)}, u32[]{:S(2)}, u32[]{:S(2)}) async-start(bf16[16,256,256]{2,1,0:T(8,128)(2,1)} %bitcast.9), calls=%async_computation | async-start | bytes 4194304 | tf_op jit(solution)/shard_map/all_to_all | solution.py:377
  114.9 0.0 copy-done.1
  114.9 0.6 copy.7
  115.5 48.3 %all-to-all-done = bf16[16,256,256]{2,1,0:T(8,128)(2,1)S(1)} async-done(((bf16[16,256,256]{2,1,0:T(8,128)(2,1)}), bf16[16,256,256]{2,1,0:T(8,128)(2,1)S(1)}, u32[]{:S(2)}, u32[]{:S(2)}) %all-to-all-start) | async-done | bytes 2097184 | tf_op jit(solution)/shard_map/all_to_all | solution.py:377
  163.8 1.0 convert_reduce_fusion
  (2 shorter events, 0.0 us)
Async XLA Ops:
  0.6 4.6 %copy-start = (bf16[4096,256]{1,0:T(8,128)(2,1)S(1)}, bf16[4096,256]{1,0:T(8,128)(2,1)}, u32[]{:S(2)}) copy-start(bf16[4096,256]{1,0:T(8,128)(2,1)} %prototypes_ref.1) | copy-start | bytes 6291460
  106.2 8.6 %copy-start.1 = (f32[8,512]{1,0:T(8,128)S(1)}, f32[8,512]{1,0:T(8,128)}, u32[]{:S(2)}) copy-start(f32[8,512]{1,0:T(8,128)} %get-tuple-element.7) | copy-start | bytes 49156
  106.2 57.6 %all-to-all-start = ((bf16[16,256,256]{2,1,0:T(8,128)(2,1)}), bf16[16,256,256]{2,1,0:T(8,128)(2,1)S(1)}, u32[]{:S(2)}, u32[]{:S(2)}) async-start(bf16[16,256,256]{2,1,0:T(8,128)(2,1)} %bitcast.9), calls=%async_computation | async-start | bytes 4194304 | tf_op jit(solution)/shard_map/all_to_all | solution.py:377

commit v8 on v7

--- a/solution.py
+++ b/solution.py
@@ -364,6 +364,69 @@
     )(*slots, slot_images, slot_protos)
 
 
+def scatter_kernel(shares_ref, out_ref, landed, send_sems, recv_sems):
+    count = lax.axis_size("img")
+    me = lax.axis_index("img")
+    barrier = pltpu.get_barrier_semaphore()
+
+    def greet(step, carry):
+        pl.semaphore_signal(barrier, inc=1, device_id={"img": lax.rem(me + step, count)},
+                            device_id_type=pl.DeviceIdType.MESH)
+        return carry
+
+    lax.fori_loop(1, count, greet, 0)
+    pl.semaphore_wait(barrier, count - 1)
+
+    def peer_copy(peer, slot, source):
+        return pltpu.make_async_remote_copy(
+            src_ref=shares_ref.at[source],
+            dst_ref=landed.at[slot],
+            send_sem=send_sems.at[peer],
+            recv_sem=recv_sems.at[slot],
+            device_id={"img": peer},
+            device_id_type=pl.DeviceIdType.MESH,
+        )
+
+    def send(step, carry):
+        peer = lax.rem(me + step, count)
+        peer_copy(peer, me, peer).start()
+        return carry
+
+    lax.fori_loop(1, count, send, 0)
+    out_ref[...] = shares_ref[me].astype(jnp.float32)
+
+    def receive(step, carry):
+        peer = lax.rem(me + count - step, count)
+        peer_copy(peer, peer, me).wait_recv()
+        out_ref[...] += landed[peer].astype(jnp.float32)
+        return carry
+
+    lax.fori_loop(1, count, receive, 0)
+
+    def drain(step, carry):
+        peer = lax.rem(me + step, count)
+        peer_copy(peer, me, peer).wait_send()
+        return carry
+
+    lax.fori_loop(1, count, drain, 0)
+
+
+def scatter_sum(shares):
+    count, rows, width = shares.shape
+    return pl.pallas_call(
+        scatter_kernel,
+        out_shape=jax.ShapeDtypeStruct((rows, width), jnp.float32),
+        in_specs=whole_specs(1),
+        out_specs=pl.BlockSpec(memory_space=pltpu.VMEM),
+        scratch_shapes=[
+            pltpu.VMEM(shares.shape, shares.dtype),
+            pltpu.SemaphoreType.DMA((count,)),
+            pltpu.SemaphoreType.DMA((count,)),
+        ],
+        compiler_params=pltpu.CompilerParams(collective_id=1, has_side_effects=True),
+    )(shares)
+
+
 def shards(images, prototypes, tile_row, tile_proto, tile_valid):
     img_count = lax.axis_size("img")
     proto_count = lax.axis_size("proto")
@@ -374,13 +437,9 @@
     row_pot, col_pot, col_columns = sinkhorn(slots, slot_images, slot_protos, log_ratio)
     partial_value = final_pass(slots, images, prototypes, col_columns, row_pot)
     img_count = lax.axis_size("img")
-    shares = lax.all_to_all(
-        partial_value.reshape(img_count, PB_DEV * TILE // img_count, E).astype(jnp.bfloat16),
-        "img",
-        0,
-        0,
+    proto_share = scatter_sum(
+        partial_value.reshape(img_count, PB_DEV * TILE // img_count, E).astype(jnp.bfloat16)
     )
-    proto_share = jnp.sum(shares.astype(jnp.float32), axis=0)
     return (proto_share, col_pot.reshape(PB_DEV * TILE))
 
 

time: 165 us -> 165 us (level)
  Pallas kernels: 94.1 us -> 149 us
  waiting for transfers between devices: 48.3 us -> 0 us
  starting transfers between devices: 8.64 us -> 0 us
  local copies, waits for them, and re-layouts: 6.88 us -> 9.38 us
    pallas_call x0 -> x1, Pallas kernels: none -> 54.1 us  [scatter_sum(): pl.pallas_call(scatter_kernel, out_shape=jax.ShapeDtypeStruct((rows, widt...]
    all_to_all x1 -> x0, waiting for transfers between devices: 48.3 us -> none  [shards(): lax.all_to_all(partial_value.reshape(img_count, PB_DEV * TILE // img_coun...]
    all_to_all x1 -> x0, starting transfers between devices: 8.64 us -> none  [shards(): lax.all_to_all(partial_value.reshape(img_count, PB_DEV * TILE // img_coun...]
    unnamed x5 -> x4, local copies, waits for them, and re-layouts: 0.62 us -> 3 us
  transfers between devices with their start and end apart: 1 -> 0, of which waited for: 1 -> 0; matrix products, arithmetic and copies ran while one was open for 0% -> 0% of each run, Pallas kernels for 0% -> 0%
where the time goes in v8:
time: 165 us; the launch traced here: 164 us
  Pallas kernels  149 us (90%)
  local copies, waits for them, and re-layouts  9.38 us (6%)
  other arithmetic  5.07 us (3%)
    pallas_call x1, Pallas kernels, sinkhorn(): pl.pallas_call(functools.partial(sinkhorn_kernel, log_ratio), out_shape=(...  88 us
    pallas_call x1, Pallas kernels, scatter_sum(): pl.pallas_call(scatter_kernel, out_shape=jax.ShapeDtypeStruct((rows, widt...  54.1 us
    pallas_call x1, Pallas kernels, final_pass(): pl.pallas_call(final_kernel, out_shape=jax.ShapeDtypeStruct((PB_DEV, TILE...  7.11 us
    convert_element_type x1, other arithmetic, shards(): partial_value.reshape(img_count, PB_DEV * TILE // img_count, E)  3.74 us

profile of v8, /device:TPU:1, one launch (start us, length us, event | category | flops | bytes accessed | tf_op | source)
XLA Modules:
  0.0 164.3 jit_solution(6638150373936095907)
XLA Ops:
  0.6 0.7 fusion
  1.3 0.7 fusion.1
  2.0 0.0 copy-start
  2.0 3.2 %gather_fusion = bf16[6,512,256]{2,1,0:T(8,128)(2,1)} fusion(bf16[4,512,256]{2,1,0:T(8,128)(2,1)} %bitcast.17, s32[1024]{0:T(1024)S(1)} %pad_clamp_fusion.1), kind=kCustom, calls=%fused_computation | custom fusion | bytes 3145752 | tf_op jit(solution)/shard_map/gather | solution.py:435
  5.2 0.0 copy-done
  5.2 1.8 %gather_fusion.1 = bf16[6,512,256]{2,1,0:T(8,128)(2,1)} fusion(bf16[8,512,256]{2,1,0:T(8,128)(2,1)S(1)} %bitcast.18, s32[1024]{0:T(1024)S(1)} %pad_clamp_fusion), kind=kCustom, calls=%fused_computation.1 | custom fusion | bytes 3145752 | tf_op jit(solution)/shard_map/gather | solution.py:436
  7.1 88.0 %shard_map.68 = (f32[4,512]{1,0:T(4,128)}, f32[8,512]{1,0:T(8,128)}, f32[8,512,1]{2,1,0:T(8,128)}) custom-call(s32[6]{0:T(128)} %bitcast.21, s32[6]{0:T(128)} %bitcast.23, s32[6]{0:T(128)} %bitcast.25, bf16[6,512,256]{2,1,0:T(8,128)(2,1)} %gather_fusion, bf16[6,512,256]{2,1,0:T(8,128)(2,1)} %gather_fusion.1), custom_call_target="tpu_custom_call" | custom-call | tf_op jit(solution)/shard_map/pallas_call | solution.py:350
  95.0 1.3 reshape.94.row_ref
  96.3 1.3 copy.7
  97.7 7.1 %shard_map.69 = f32[8,512,256]{2,1,0:T(8,128)} custom-call(s32[6]{0:T(128)} %bitcast.22, s32[6]{0:T(128)} %bitcast.24, s32[6]{0:T(128)} %bitcast.26, bf16[2048,256]{1,0:T(8,128)(2,1)} %images_ref.1, bf16[4096,256]{1,0:T(8,128)(2,1)} %prototypes_ref.1, f32[8,512,1]{2,1,0:T(8,128)} %get-tuple-element.5.col_ref, f32[4,1,512]{2,1,0:T(1,128)} %reshape.94.row_ref), custom_call_target="tpu_custom_call" | custom-call | tf_op jit(solution)/shard_map/pallas_call | solution.py:183
  104.8 3.7 %convert_element_type.5 = bf16[8,512,256]{2,1,0:T(8,128)(2,1)} convert(f32[8,512,256]{2,1,0:T(8,128)} %shard_map.69) | non-fusion elementwise | flops 1048576 | bytes 6291456 | tf_op jit(solution)/shard_map/convert_element_type | solution.py:441
  108.5 54.1 %shard_map.70 = f32[256,256]{1,0:T(8,128)} custom-call(bf16[16,256,256]{2,1,0:T(8,128)(2,1)} %bitcast.16), custom_call_target="tpu_custom_call" | custom-call | tf_op jit(solution)/shard_map/pallas_call | solution.py:416
  162.6 1.7 %copy.9 = f32[256,256]{1,0:T(8,128)} copy(f32[256,256]{1,0:T(8,128)} %shard_map.70) | data formatting | bytes 524288
  (2 shorter events, 0.0 us)
Async XLA Ops:
  2.0 3.2 %copy-start = (bf16[4096,256]{1,0:T(8,128)(2,1)S(1)}, bf16[4096,256]{1,0:T(8,128)(2,1)}, u32[]{:S(2)}) copy-start(bf16[4096,256]{1,0:T(8,128)(2,1)} %prototypes_ref.1) | copy-start | bytes 6291460

commit v9 on v8

--- a/solution.py
+++ b/solution.py
@@ -364,64 +364,89 @@
     )(*slots, slot_images, slot_protos)
 
 
-def scatter_kernel(shares_ref, out_ref, landed, send_sems, recv_sems):
+def scatter_kernel(shares_ref, out_ref, paired, pair_sums, landed, pair_sems, send_sems,
+                   recv_sems):
     count = lax.axis_size("img")
+    chips = count // 2
     me = lax.axis_index("img")
+    core = lax.rem(me, 2)
+    chip = me // 2
+    partner = me + 1 - 2 * core
     barrier = pltpu.get_barrier_semaphore()
+    pl.semaphore_signal(barrier, inc=1, device_id={"img": partner},
+                        device_id_type=pl.DeviceIdType.MESH)
 
     def greet(step, carry):
-        pl.semaphore_signal(barrier, inc=1, device_id={"img": lax.rem(me + step, count)},
+        peer = lax.rem(chip + step, chips) * 2 + core
+        pl.semaphore_signal(barrier, inc=1, device_id={"img": peer},
                             device_id_type=pl.DeviceIdType.MESH)
         return carry
 
-    lax.fori_loop(1, count, greet, 0)
-    pl.semaphore_wait(barrier, count - 1)
-
-    def peer_copy(peer, slot, source):
+    lax.fori_loop(1, chips, greet, 0)
+    pl.semaphore_wait(barrier, chips)
+
+    pair_copy = pltpu.make_async_remote_copy(
+        src_ref=shares_ref.at[1 - core],
+        dst_ref=paired,
+        send_sem=pair_sems.at[0],
+        recv_sem=pair_sems.at[1],
+        device_id={"img": partner},
+        device_id_type=pl.DeviceIdType.MESH,
+    )
+    pair_copy.start()
+    pair_copy.wait_recv()
+    pair_sums[...] = (
+        shares_ref[core].astype(jnp.float32) + paired[...].astype(jnp.float32)
+    ).astype(jnp.bfloat16)
+    pair_copy.wait_send()
+
+    def peer_copy(peer_chip, slot):
         return pltpu.make_async_remote_copy(
-            src_ref=shares_ref.at[source],
+            src_ref=pair_sums.at[peer_chip],
             dst_ref=landed.at[slot],
-            send_sem=send_sems.at[peer],
+            send_sem=send_sems.at[peer_chip],
             recv_sem=recv_sems.at[slot],
-            device_id={"img": peer},
+            device_id={"img": peer_chip * 2 + core},
             device_id_type=pl.DeviceIdType.MESH,
         )
 
     def send(step, carry):
-        peer = lax.rem(me + step, count)
-        peer_copy(peer, me, peer).start()
-        return carry
-
-    lax.fori_loop(1, count, send, 0)
-    out_ref[...] = shares_ref[me].astype(jnp.float32)
+        peer_copy(lax.rem(chip + step, chips), chip).start()
+        return carry
+
+    lax.fori_loop(1, chips, send, 0)
+    out_ref[...] = pair_sums[chip].astype(jnp.float32)
 
     def receive(step, carry):
-        peer = lax.rem(me + count - step, count)
-        peer_copy(peer, peer, me).wait_recv()
-        out_ref[...] += landed[peer].astype(jnp.float32)
-        return carry
-
-    lax.fori_loop(1, count, receive, 0)
+        source = lax.rem(chip + chips - step, chips)
+        peer_copy(source, source).wait_recv()
+        out_ref[...] += landed[source].astype(jnp.float32)
+        return carry
+
+    lax.fori_loop(1, chips, receive, 0)
 
     def drain(step, carry):
-        peer = lax.rem(me + step, count)
-        peer_copy(peer, me, peer).wait_send()
-        return carry
-
-    lax.fori_loop(1, count, drain, 0)
+        peer_copy(lax.rem(chip + step, chips), chip).wait_send()
+        return carry
+
+    lax.fori_loop(1, chips, drain, 0)
 
 
 def scatter_sum(shares):
-    count, rows, width = shares.shape
+    cores, chips, rows, width = shares.shape
+    half = (chips, rows, width)
     return pl.pallas_call(
         scatter_kernel,
         out_shape=jax.ShapeDtypeStruct((rows, width), jnp.float32),
         in_specs=whole_specs(1),
         out_specs=pl.BlockSpec(memory_space=pltpu.VMEM),
         scratch_shapes=[
-            pltpu.VMEM(shares.shape, shares.dtype),
-            pltpu.SemaphoreType.DMA((count,)),
-            pltpu.SemaphoreType.DMA((count,)),
+            pltpu.VMEM(half, shares.dtype),
+            pltpu.VMEM(half, shares.dtype),
+            pltpu.VMEM(half, shares.dtype),
+            pltpu.SemaphoreType.DMA((2,)),
+            pltpu.SemaphoreType.DMA((chips,)),
+            pltpu.SemaphoreType.DMA((chips,)),
         ],
         compiler_params=pltpu.CompilerParams(collective_id=1, has_side_effects=True),
     )(shares)
@@ -437,9 +462,8 @@
     row_pot, col_pot, col_columns = sinkhorn(slots, slot_images, slot_protos, log_ratio)
     partial_value = final_pass(slots, images, prototypes, col_columns, row_pot)
     img_count = lax.axis_size("img")
-    proto_share = scatter_sum(
-        partial_value.reshape(img_count, PB_DEV * TILE // img_count, E).astype(jnp.bfloat16)
-    )
+    by_core = partial_value.reshape(img_count // 2, 2, PB_DEV * TILE // img_count, E)
+    proto_share = scatter_sum(jnp.swapaxes(by_core, 0, 1).astype(jnp.bfloat16))
     return (proto_share, col_pot.reshape(PB_DEV * TILE))
 
 

time: 165 us -> 145 us (0.88)
  Pallas kernels: 149 us -> 130 us
    pallas_call x1, Pallas kernels: 54.1 us -> 34 us  [scatter_sum(): pl.pallas_call(scatter_kernel, out_shape=jax.ShapeDtypeStruct((rows, widt...]
where the time goes in v9:
time: 145 us
  Pallas kernels  130 us (90%)
  local copies, waits for them, and re-layouts  10.9 us (8%)
  other arithmetic  3.75 us (3%)
    pallas_call x1, Pallas kernels, sinkhorn(): pl.pallas_call(functools.partial(sinkhorn_kernel, log_ratio), out_shape=(...  88 us
    pallas_call x1, Pallas kernels, scatter_sum(): pl.pallas_call(scatter_kernel, out_shape=jax.ShapeDtypeStruct((rows, widt...  34 us
    pallas_call x1, Pallas kernels, final_pass(): pl.pallas_call(final_kernel, out_shape=jax.ShapeDtypeStruct((PB_DEV, TILE...  7.91 us
    gather x1, local copies, waits for them, and re-layouts, shards(): slot_images = images.reshape(RB_DEV, TILE, E)[slots[0]]  3.23 us
    unnamed x4, local copies, waits for them, and re-layouts  3 us

profile of v9, /device:TPU:1, one launch (start us, length us, event | category | flops | bytes accessed | tf_op | source)
XLA Modules:
  0.0 145.1 jit_solution(17922375528681877066)
XLA Ops:
  0.6 0.7 fusion
  1.3 0.7 fusion.1
  2.0 0.0 copy-start
  2.0 3.2 %gather_fusion = bf16[6,512,256]{2,1,0:T(8,128)(2,1)} fusion(bf16[4,512,256]{2,1,0:T(8,128)(2,1)} %bitcast.21, s32[1024]{0:T(1024)S(1)} %pad_clamp_fusion.1), kind=kCustom, calls=%fused_computation | custom fusion | bytes 3145752 | tf_op jit(solution)/shard_map/gather | solution.py:460
  5.2 0.0 copy-done
  5.2 1.8 %gather_fusion.1 = bf16[6,512,256]{2,1,0:T(8,128)(2,1)} fusion(bf16[8,512,256]{2,1,0:T(8,128)(2,1)S(1)} %bitcast.22, s32[1024]{0:T(1024)S(1)} %pad_clamp_fusion), kind=kCustom, calls=%fused_computation.1 | custom fusion | bytes 3145752 | tf_op jit(solution)/shard_map/gather | solution.py:461
  7.1 88.0 %shard_map.68 = (f32[4,512]{1,0:T(4,128)}, f32[8,512]{1,0:T(8,128)}, f32[8,512,1]{2,1,0:T(8,128)}) custom-call(s32[6]{0:T(128)} %bitcast.25, s32[6]{0:T(128)} %bitcast.27, s32[6]{0:T(128)} %bitcast.29, bf16[6,512,256]{2,1,0:T(8,128)(2,1)} %gather_fusion, bf16[6,512,256]{2,1,0:T(8,128)(2,1)} %gather_fusion.1), custom_call_target="tpu_custom_call" | custom-call | tf_op jit(solution)/shard_map/pallas_call | solution.py:350
  95.0 1.3 reshape.94.row_ref
  96.3 1.3 copy.8
  97.7 7.9 %shard_map.69 = f32[8,512,256]{2,1,0:T(8,128)} custom-call(s32[6]{0:T(128)} %bitcast.26, s32[6]{0:T(128)} %bitcast.28, s32[6]{0:T(128)} %bitcast.30, bf16[2048,256]{1,0:T(8,128)(2,1)} %images_ref.1, bf16[4096,256]{1,0:T(8,128)(2,1)} %prototypes_ref.1, f32[8,512,1]{2,1,0:T(8,128)} %get-tuple-element.5.col_ref, f32[4,1,512]{2,1,0:T(1,128)} %reshape.94.row_ref), custom_call_target="tpu_custom_call" | custom-call | tf_op jit(solution)/shard_map/pallas_call | solution.py:183
  105.6 2.4 %convert_element_type.7 = bf16[8,512,256]{2,1,0:T(8,128)(2,1)S(1)} convert(f32[8,512,256]{2,1,0:T(8,128)} %shard_map.69) | non-fusion elementwise | flops 1048576 | bytes 6291456 | tf_op jit(solution)/shard_map/convert_element_type | solution.py:466
  108.0 1.5 %copy.10 = bf16[8,2,256,256]{3,2,0,1:T(8,128)(2,1)} copy(bf16[8,2,256,256]{3,2,1,0:T(8,128)(2,1)S(1)} %bitcast.19) | data formatting | bytes 4194304 | tf_op jit(solution)/shard_map/convert_element_type | solution.py:466
  109.5 34.0 %shard_map.70 = f32[256,256]{1,0:T(8,128)} custom-call(bf16[2,8,256,256]{3,2,1,0:T(8,128)(2,1)} %bitcast.20), custom_call_target="tpu_custom_call" | custom-call | tf_op jit(solution)/shard_map/pallas_call | solution.py:438
  143.4 1.7 %copy.12 = f32[256,256]{1,0:T(8,128)} copy(f32[256,256]{1,0:T(8,128)} %shard_map.70) | data formatting | bytes 524288
  (2 shorter events, 0.0 us)
Async XLA Ops:
  2.0 3.2 %copy-start = (bf16[4096,256]{1,0:T(8,128)(2,1)S(1)}, bf16[4096,256]{1,0:T(8,128)(2,1)}, u32[]{:S(2)}) copy-start(bf16[4096,256]{1,0:T(8,128)(2,1)} %prototypes_ref.1) | copy-start | bytes 6291460

commit v10 on v9

--- a/solution.py
+++ b/solution.py
@@ -159,8 +159,8 @@
 
 
 def final_kernel(rows_ref, protos_ref, valid_ref, images_ref, prototypes_ref,
-                 col_ref, row_ref, out_ref):
-    out_ref[...] = jnp.zeros(out_ref.shape, jnp.float32)
+                 col_ref, row_ref, shares_ref, acc_ref):
+    acc_ref[...] = jnp.zeros(acc_ref.shape, jnp.float32)
     score_scale = float(E) ** (-0.5)
     for position in range(MAXT):
 
@@ -176,16 +176,24 @@
             weights = jnp.exp(
                 products * score_scale + col_ref[proto_block] + row_ref[row_block]
             ).astype(jnp.bfloat16)
-            out_ref[proto_block] += jnp.dot(weights, rows_here, preferred_element_type=jnp.float32)
+            acc_ref[proto_block] += jnp.dot(weights, rows_here, preferred_element_type=jnp.float32)
+
+    half = TILE // 2
+    for block in range(PB_DEV):
+        for core in range(2):
+            shares_ref[core, block] = acc_ref[block, core * half:(core + 1) * half, :].astype(
+                jnp.bfloat16
+            )
 
 
 def final_pass(slots, images, prototypes, col_column, row_pot):
     return pl.pallas_call(
         final_kernel,
-        out_shape=jax.ShapeDtypeStruct((PB_DEV, TILE, E), jnp.float32),
+        out_shape=jax.ShapeDtypeStruct((2, PB_DEV, TILE // 2, E), jnp.bfloat16),
         in_specs=slot_specs() + whole_specs(4),
         out_specs=pl.BlockSpec(memory_space=pltpu.VMEM),
-    )(*slots, images, prototypes, col_column, row_pot.reshape(RB_DEV, 1, TILE))
+        scratch_shapes=[pltpu.VMEM((PB_DEV, TILE, E), jnp.float32)],
+    )(*slots, images, prototypes, col_column, row_pot)
 
 
 def to_column(lanes):
@@ -332,7 +340,8 @@
                           col_refs[0:2], col_refs[2:4], col_refs[4:6])
         col_pot = -merged
         col_t = to_column(col_pot)
-    row_out[...] = row_pot
+    for block in range(RB_DEV):
+        row_out[block] = row_pot[block:block + 1]
     col_out[...] = col_pot
     for block in range(PB_DEV):
         col_columns_out[block] = col_t[:, block:block + 1]
@@ -350,7 +359,7 @@
     return pl.pallas_call(
         functools.partial(sinkhorn_kernel, log_ratio),
         out_shape=(
-            jax.ShapeDtypeStruct((RB_DEV, TILE), jnp.float32),
+            jax.ShapeDtypeStruct((RB_DEV, 1, TILE), jnp.float32),
             jax.ShapeDtypeStruct((PB_DEV, TILE), jnp.float32),
             jax.ShapeDtypeStruct((PB_DEV, TILE, 1), jnp.float32),
         ),
@@ -461,9 +470,7 @@
     slot_protos = prototypes.reshape(PB_DEV, TILE, E)[slots[1]]
     row_pot, col_pot, col_columns = sinkhorn(slots, slot_images, slot_protos, log_ratio)
     partial_value = final_pass(slots, images, prototypes, col_columns, row_pot)
-    img_count = lax.axis_size("img")
-    by_core = partial_value.reshape(img_count // 2, 2, PB_DEV * TILE // img_count, E)
-    proto_share = scatter_sum(jnp.swapaxes(by_core, 0, 1).astype(jnp.bfloat16))
+    proto_share = scatter_sum(partial_value)
     return (proto_share, col_pot.reshape(PB_DEV * TILE))
 
 

time: 145 us -> 141 us (0.972)
  local copies, waits for them, and re-layouts: 10.9 us -> 7.37 us
  other arithmetic: 3.75 us -> 1.33 us
    pallas_call x1, Pallas kernels: 34 us -> 36.9 us  [scatter_sum(): pl.pallas_call(scatter_kernel, out_shape=jax.ShapeDtypeStruct((rows, widt...]
    convert_element_type x1 -> x0, other arithmetic: 2.42 us -> none  [shards(): proto_share = scatter_sum(jnp.swapaxes(by_core, 0, 1).astype(jnp.bfloat16))]
    pallas_call x1, Pallas kernels: 7.91 us -> 6.34 us  [final_pass(): pl.pallas_call(final_kernel, out_shape=jax.ShapeDtypeStruct((2, PB_DEV, T...]
    convert_element_type x1 -> x0, local copies, waits for them, and re-layouts: 1.49 us -> none  [shards(): proto_share = scatter_sum(jnp.swapaxes(by_core, 0, 1).astype(jnp.bfloat16))]
    unnamed x4 -> x6, local copies, waits for them, and re-layouts: 3 us -> 2.29 us
where the time goes in v10:
time: 141 us
  Pallas kernels  131 us (93%)
  local copies, waits for them, and re-layouts  7.37 us (5%)
    pallas_call x1, Pallas kernels, sinkhorn(): pl.pallas_call(functools.partial(sinkhorn_kernel, log_ratio), out_shape=(...  88.1 us
    pallas_call x1, Pallas kernels, scatter_sum(): pl.pallas_call(scatter_kernel, out_shape=jax.ShapeDtypeStruct((rows, widt...  36.9 us
    pallas_call x1, Pallas kernels, final_pass(): pl.pallas_call(final_kernel, out_shape=jax.ShapeDtypeStruct((2, PB_DEV, T...  6.34 us
    gather x1, local copies, waits for them, and re-layouts, shards(): slot_images = images.reshape(RB_DEV, TILE, E)[slots[0]]  3.23 us

profile of v10, /device:TPU:1, one launch (start us, length us, event | category | flops | bytes accessed | tf_op | source)
XLA Modules:
  0.0 140.7 jit_solution(7234728854474993768)
XLA Ops:
  0.6 0.7 fusion
  1.3 0.7 fusion.1
  2.0 0.0 copy-start
  2.0 3.2 %gather_fusion = bf16[6,512,256]{2,1,0:T(8,128)(2,1)} fusion(bf16[4,512,256]{2,1,0:T(8,128)(2,1)} %bitcast.15, s32[1024]{0:T(1024)S(1)} %pad_clamp_fusion.1), kind=kCustom, calls=%fused_computation | custom fusion | bytes 3145752 | tf_op jit(solution)/shard_map/gather | solution.py:469
  5.2 0.0 copy-done
  5.2 1.9 %gather_fusion.1 = bf16[6,512,256]{2,1,0:T(8,128)(2,1)} fusion(bf16[8,512,256]{2,1,0:T(8,128)(2,1)S(1)} %bitcast.16, s32[1024]{0:T(1024)S(1)} %pad_clamp_fusion), kind=kCustom, calls=%fused_computation.1 | custom fusion | bytes 3145752 | tf_op jit(solution)/shard_map/gather | solution.py:470
  7.1 88.1 %shard_map.68 = (f32[4,1,512]{2,1,0:T(1,128)}, f32[8,512]{1,0:T(8,128)}, f32[8,512,1]{2,1,0:T(8,128)}) custom-call(s32[6]{0:T(128)} %bitcast.19, s32[6]{0:T(128)} %bitcast.21, s32[6]{0:T(128)} %bitcast.23, bf16[6,512,256]{2,1,0:T(8,128)(2,1)} %gather_fusion, bf16[6,512,256]{2,1,0:T(8,128)(2,1)} %gather_fusion.1), custom_call_target="tpu_custom_call" | custom-call | tf_op jit(solution)/shard_map/pallas_call | solution.py:359
  95.1 6.3 %shard_map.69.shares_ref = bf16[2,8,256,256]{3,2,1,0:T(8,128)(2,1)} custom-call(s32[6]{0:T(128)} %bitcast.20, s32[6]{0:T(128)} %bitcast.22, s32[6]{0:T(128)} %bitcast.24, bf16[2048,256]{1,0:T(8,128)(2,1)} %images_ref.1, bf16[4096,256]{1,0:T(8,128)(2,1)} %prototypes_ref.1, f32[8,512,1]{2,1,0:T(8,128)} %get-tuple-element.5.col_ref, ...), custom_call_target="tpu_custom_call" | custom-call | tf_op jit(solution)/shard_map/pallas_call | solution.py:190
  101.5 0.0 copy-start.1
  101.5 36.9 %shard_map.70 = f32[256,256]{1,0:T(8,128)} custom-call(bf16[2,8,256,256]{3,2,1,0:T(8,128)(2,1)} %shard_map.69.shares_ref), custom_call_target="tpu_custom_call" | custom-call | tf_op jit(solution)/shard_map/pallas_call | solution.py:447
  138.4 0.0 copy-done.1
  138.4 0.6 copy.7
  139.0 1.7 %copy.9 = f32[256,256]{1,0:T(8,128)} copy(f32[256,256]{1,0:T(8,128)} %shard_map.70) | data formatting | bytes 524288
  (2 shorter events, 0.0 us)
Async XLA Ops:
  2.0 3.2 %copy-start = (bf16[4096,256]{1,0:T(8,128)(2,1)S(1)}, bf16[4096,256]{1,0:T(8,128)(2,1)}, u32[]{:S(2)}) copy-start(bf16[4096,256]{1,0:T(8,128)(2,1)} %prototypes_ref.1) | copy-start | bytes 6291460
  101.5 36.9 %copy-start.1 = (f32[8,512]{1,0:T(8,128)S(1)}, f32[8,512]{1,0:T(8,128)}, u32[]{:S(2)}) copy-start(f32[8,512]{1,0:T(8,128)} %get-tuple-element.7) | copy-start | bytes 49156

commit v11 on v10

--- a/solution.py
+++ b/solution.py
@@ -394,20 +394,15 @@
     lax.fori_loop(1, chips, greet, 0)
     pl.semaphore_wait(barrier, chips)
 
-    pair_copy = pltpu.make_async_remote_copy(
-        src_ref=shares_ref.at[1 - core],
-        dst_ref=paired,
-        send_sem=pair_sems.at[0],
-        recv_sem=pair_sems.at[1],
-        device_id={"img": partner},
-        device_id_type=pl.DeviceIdType.MESH,
-    )
-    pair_copy.start()
-    pair_copy.wait_recv()
-    pair_sums[...] = (
-        shares_ref[core].astype(jnp.float32) + paired[...].astype(jnp.float32)
-    ).astype(jnp.bfloat16)
-    pair_copy.wait_send()
+    def pair_copy(piece):
+        return pltpu.make_async_remote_copy(
+            src_ref=shares_ref.at[1 - core, piece],
+            dst_ref=paired.at[piece],
+            send_sem=pair_sems.at[0, piece],
+            recv_sem=pair_sems.at[1, piece],
+            device_id={"img": partner},
+            device_id_type=pl.DeviceIdType.MESH,
+        )
 
     def peer_copy(peer_chip, slot):
         return pltpu.make_async_remote_copy(
@@ -419,11 +414,26 @@
             device_id_type=pl.DeviceIdType.MESH,
         )
 
+    def pair_send(step, carry):
+        pair_copy(lax.rem(chip + step, chips)).start()
+        return carry
+
+    lax.fori_loop(1, chips + 1, pair_send, 0)
+
+    def add_pair(piece):
+        pair_copy(piece).wait_recv()
+        pair_sums[piece] = (
+            shares_ref[core, piece].astype(jnp.float32) + paired[piece].astype(jnp.float32)
+        ).astype(jnp.bfloat16)
+
     def send(step, carry):
-        peer_copy(lax.rem(chip + step, chips), chip).start()
+        piece = lax.rem(chip + step, chips)
+        add_pair(piece)
+        peer_copy(piece, chip).start()
         return carry
 
     lax.fori_loop(1, chips, send, 0)
+    add_pair(chip)
     out_ref[...] = pair_sums[chip].astype(jnp.float32)
 
     def receive(step, carry):
@@ -439,6 +449,12 @@
         return carry
 
     lax.fori_loop(1, chips, drain, 0)
+
+    def pair_drain(step, carry):
+        pair_copy(lax.rem(chip + step, chips)).wait_send()
+        return carry
+
+    lax.fori_loop(1, chips + 1, pair_drain, 0)
 
 
 def scatter_sum(shares):
@@ -453,7 +469,7 @@
             pltpu.VMEM(half, shares.dtype),
             pltpu.VMEM(half, shares.dtype),
             pltpu.VMEM(half, shares.dtype),
-            pltpu.SemaphoreType.DMA((2,)),
+            pltpu.SemaphoreType.DMA((2, chips)),
             pltpu.SemaphoreType.DMA((chips,)),
             pltpu.SemaphoreType.DMA((chips,)),
         ],

time: 141 us -> 138 us (0.979)
  Pallas kernels: 131 us -> 129 us
    pallas_call x1, Pallas kernels: 36.9 us -> 34.4 us  [scatter_sum(): pl.pallas_call(scatter_kernel, out_shape=jax.ShapeDtypeStruct((rows, widt...]
where the time goes in v11:
time: 138 us
  Pallas kernels  129 us (93%)
  local copies, waits for them, and re-layouts  7.37 us (5%)
    pallas_call x1, Pallas kernels, sinkhorn(): pl.pallas_call(functools.partial(sinkhorn_kernel, log_ratio), out_shape=(...  88.1 us
    pallas_call x1, Pallas kernels, scatter_sum(): pl.pallas_call(scatter_kernel, out_shape=jax.ShapeDtypeStruct((rows, widt...  34.4 us
    pallas_call x1, Pallas kernels, final_pass(): pl.pallas_call(final_kernel, out_shape=jax.ShapeDtypeStruct((2, PB_DEV, T...  6.34 us
    gather x1, local copies, waits for them, and re-layouts, shards(): slot_images = images.reshape(RB_DEV, TILE, E)[slots[0]]  3.23 us

profile of v11, /device:TPU:1, one launch (start us, length us, event | category | flops | bytes accessed | tf_op | source)
XLA Modules:
  0.0 138.2 jit_solution(7180076304546627020)
XLA Ops:
  0.6 0.7 fusion
  1.3 0.7 fusion.1
  2.0 0.0 copy-start
  2.0 3.2 %gather_fusion = bf16[6,512,256]{2,1,0:T(8,128)(2,1)} fusion(bf16[4,512,256]{2,1,0:T(8,128)(2,1)} %bitcast.15, s32[1024]{0:T(1024)S(1)} %pad_clamp_fusion.1), kind=kCustom, calls=%fused_computation | custom fusion | bytes 3145752 | tf_op jit(solution)/shard_map/gather | solution.py:485
  5.2 0.0 copy-done
  5.2 1.9 %gather_fusion.1 = bf16[6,512,256]{2,1,0:T(8,128)(2,1)} fusion(bf16[8,512,256]{2,1,0:T(8,128)(2,1)S(1)} %bitcast.16, s32[1024]{0:T(1024)S(1)} %pad_clamp_fusion), kind=kCustom, calls=%fused_computation.1 | custom fusion | bytes 3145752 | tf_op jit(solution)/shard_map/gather | solution.py:486
  7.1 88.1 %shard_map.68 = (f32[4,1,512]{2,1,0:T(1,128)}, f32[8,512]{1,0:T(8,128)}, f32[8,512,1]{2,1,0:T(8,128)}) custom-call(s32[6]{0:T(128)} %bitcast.19, s32[6]{0:T(128)} %bitcast.21, s32[6]{0:T(128)} %bitcast.23, bf16[6,512,256]{2,1,0:T(8,128)(2,1)} %gather_fusion, bf16[6,512,256]{2,1,0:T(8,128)(2,1)} %gather_fusion.1), custom_call_target="tpu_custom_call" | custom-call | tf_op jit(solution)/shard_map/pallas_call | solution.py:359
  95.1 6.3 %shard_map.69.shares_ref = bf16[2,8,256,256]{3,2,1,0:T(8,128)(2,1)} custom-call(s32[6]{0:T(128)} %bitcast.20, s32[6]{0:T(128)} %bitcast.22, s32[6]{0:T(128)} %bitcast.24, bf16[2048,256]{1,0:T(8,128)(2,1)} %images_ref.1, bf16[4096,256]{1,0:T(8,128)(2,1)} %prototypes_ref.1, f32[8,512,1]{2,1,0:T(8,128)} %get-tuple-element.5.col_ref, ...), custom_call_target="tpu_custom_call" | custom-call | tf_op jit(solution)/shard_map/pallas_call | solution.py:190
  101.5 0.0 copy-start.1
  101.5 34.4 %shard_map.70 = f32[256,256]{1,0:T(8,128)} custom-call(bf16[2,8,256,256]{3,2,1,0:T(8,128)(2,1)} %shard_map.69.shares_ref), custom_call_target="tpu_custom_call" | custom-call | tf_op jit(solution)/shard_map/pallas_call | solution.py:463
  135.9 0.0 copy-done.1
  135.9 0.6 copy.7
  136.5 1.7 %copy.9 = f32[256,256]{1,0:T(8,128)} copy(f32[256,256]{1,0:T(8,128)} %shard_map.70) | data formatting | bytes 524288
  (2 shorter events, 0.0 us)
Async XLA Ops:
  2.0 3.2 %copy-start = (bf16[4096,256]{1,0:T(8,128)(2,1)S(1)}, bf16[4096,256]{1,0:T(8,128)(2,1)}, u32[]{:S(2)}) copy-start(bf16[4096,256]{1,0:T(8,128)(2,1)} %prototypes_ref.1) | copy-start | bytes 6291460
  101.5 34.5 %copy-start.1 = (f32[8,512]{1,0:T(8,128)S(1)}, f32[8,512]{1,0:T(8,128)}, u32[]{:S(2)}) copy-start(f32[8,512]{1,0:T(8,128)} %get-tuple-element.7) | copy-start | bytes 49156

commit v12 on v11

--- a/solution.py
+++ b/solution.py
@@ -262,7 +262,7 @@
 
 
 def local_merge(along_rows, rows_ref, protos_ref, valid_ref, slot_images_ref, slot_protos_ref,
-                other_columns):
+                other_columns, cache, fill):
     blocks = RB_DEV if along_rows else PB_DEV
     other_blocks = PB_DEV if along_rows else RB_DEV
     tops = [jnp.full((1, TILE), far_below, jnp.float32) for _ in range(blocks)]
@@ -278,10 +278,14 @@
             first, second, other_block, target = protos_here, rows_here, proto_block, row_block
         else:
             first, second, other_block, target = rows_here, protos_here, row_block, proto_block
-        products = lax.dot_general(
-            first, second, (((1,), (1,)), ((), ())), preferred_element_type=jnp.float32
-        )
-        values = products * score_scale + pick_column(other_columns, other_block, other_blocks)
+        if fill:
+            scores = lax.dot_general(
+                first, second, (((1,), (1,)), ((), ())), preferred_element_type=jnp.float32
+            ) * score_scale
+            cache[position] = scores
+        else:
+            scores = cache[position]
+        values = scores + pick_column(other_columns, other_block, other_blocks)
         local_top = jnp.max(values, axis=0, keepdims=True)
         local_mass = jnp.sum(jnp.exp(values - local_top), axis=0, keepdims=True)
         for block in range(blocks):
@@ -307,7 +311,8 @@
 
 
 def sinkhorn_kernel(log_ratio, rows_ref, protos_ref, valid_ref, images_ref, prototypes_ref,
-                    row_out, col_out, col_columns_out, row_packed, col_packed, *stage_refs):
+                    row_out, col_out, col_columns_out, row_cache, col_cache, row_packed,
+                    col_packed, *stage_refs):
     groups = axis_groups()
     row_refs = stage_refs[0:6]
     col_refs = stage_refs[6:12]
@@ -329,13 +334,13 @@
     col_t = jnp.zeros((TILE, PB_DEV), jnp.float32)
     for iteration in range(ITERS):
         local = local_merge(True, rows_ref, protos_ref, valid_ref, images_ref, prototypes_ref,
-                            col_t)
+                            col_t, row_cache, iteration == 0)
         merged = exchange("proto", groups["proto"], iteration, local, row_packed,
                           row_refs[0:2], row_refs[2:4], row_refs[4:6])
         row_pot = log_ratio - merged
         row_t = to_column(row_pot)
         local = local_merge(False, rows_ref, protos_ref, valid_ref, images_ref, prototypes_ref,
-                            row_t)
+                            row_t, col_cache, iteration == 0)
         merged = exchange("img", groups["img"], iteration, local, col_packed,
                           col_refs[0:2], col_refs[2:4], col_refs[4:6])
         col_pot = -merged
@@ -366,6 +371,8 @@
         in_specs=slot_specs() + whole_specs(2),
         out_specs=tuple(whole_specs(3)),
         scratch_shapes=[
+            vmem((MAXT, TILE, TILE), jnp.float32),
+            vmem((MAXT, TILE, TILE), jnp.float32),
             vmem((RB_DEV, TILE), jnp.float32),
             vmem((PB_DEV, TILE), jnp.float32),
         ] + stage_scratch,

time: 138 us -> 137 us (level)
  no operation moved by 1% of the time
where the time goes in v12:
time: 137 us
  Pallas kernels  128 us (93%)
  local copies, waits for them, and re-layouts  7.37 us (5%)
    pallas_call x1, Pallas kernels, sinkhorn(): pl.pallas_call(functools.partial(sinkhorn_kernel, log_ratio), out_shape=(...  87.4 us
    pallas_call x1, Pallas kernels, scatter_sum(): pl.pallas_call(scatter_kernel, out_shape=jax.ShapeDtypeStruct((rows, widt...  34.1 us
    pallas_call x1, Pallas kernels, final_pass(): pl.pallas_call(final_kernel, out_shape=jax.ShapeDtypeStruct((2, PB_DEV, T...  6.12 us
    gather x1, local copies, waits for them, and re-layouts, shards(): slot_images = images.reshape(RB_DEV, TILE, E)[slots[0]]  3.23 us

profile of v12, /device:TPU:1, one launch (start us, length us, event | category | flops | bytes accessed | tf_op | source)
XLA Modules:
  0.0 137.0 jit_solution(9949674943435357573)
XLA Ops:
  0.6 0.7 fusion
  1.3 0.7 fusion.1
  2.0 0.0 copy-start
  2.0 3.2 %gather_fusion = bf16[6,512,256]{2,1,0:T(8,128)(2,1)} fusion(bf16[4,512,256]{2,1,0:T(8,128)(2,1)} %bitcast.15, s32[1024]{0:T(1024)S(1)} %pad_clamp_fusion.1), kind=kCustom, calls=%fused_computation | custom fusion | bytes 3145752 | tf_op jit(solution)/shard_map/gather | solution.py:492
  5.2 0.0 copy-done
  5.2 1.9 %gather_fusion.1 = bf16[6,512,256]{2,1,0:T(8,128)(2,1)} fusion(bf16[8,512,256]{2,1,0:T(8,128)(2,1)S(1)} %bitcast.16, s32[1024]{0:T(1024)S(1)} %pad_clamp_fusion), kind=kCustom, calls=%fused_computation.1 | custom fusion | bytes 3145752 | tf_op jit(solution)/shard_map/gather | solution.py:493
  7.1 87.4 %shard_map.68 = (f32[4,1,512]{2,1,0:T(1,128)}, f32[8,512]{1,0:T(8,128)}, f32[8,512,1]{2,1,0:T(8,128)}) custom-call(s32[6]{0:T(128)} %bitcast.19, s32[6]{0:T(128)} %bitcast.21, s32[6]{0:T(128)} %bitcast.23, bf16[6,512,256]{2,1,0:T(8,128)(2,1)} %gather_fusion, bf16[6,512,256]{2,1,0:T(8,128)(2,1)} %gather_fusion.1), custom_call_target="tpu_custom_call" | custom-call | tf_op jit(solution)/shard_map/pallas_call | solution.py:364
  94.5 6.1 %shard_map.69.shares_ref = bf16[2,8,256,256]{3,2,1,0:T(8,128)(2,1)} custom-call(s32[6]{0:T(128)} %bitcast.20, s32[6]{0:T(128)} %bitcast.22, s32[6]{0:T(128)} %bitcast.24, bf16[2048,256]{1,0:T(8,128)(2,1)} %images_ref.1, bf16[4096,256]{1,0:T(8,128)(2,1)} %prototypes_ref.1, f32[8,512,1]{2,1,0:T(8,128)} %get-tuple-element.5.col_ref, ...), custom_call_target="tpu_custom_call" | custom-call | tf_op jit(solution)/shard_map/pallas_call | solution.py:190
  100.6 0.0 copy-start.1
  100.6 34.1 %shard_map.70 = f32[256,256]{1,0:T(8,128)} custom-call(bf16[2,8,256,256]{3,2,1,0:T(8,128)(2,1)} %shard_map.69.shares_ref), custom_call_target="tpu_custom_call" | custom-call | tf_op jit(solution)/shard_map/pallas_call | solution.py:470
  134.7 0.0 copy-done.1
  134.7 0.6 copy.7
  135.3 1.7 %copy.9 = f32[256,256]{1,0:T(8,128)} copy(f32[256,256]{1,0:T(8,128)} %shard_map.70) | data formatting | bytes 524288
  (2 shorter events, 0.0 us)
Async XLA Ops:
  2.0 3.2 %copy-start = (bf16[4096,256]{1,0:T(8,128)(2,1)S(1)}, bf16[4096,256]{1,0:T(8,128)(2,1)}, u32[]{:S(2)}) copy-start(bf16[4096,256]{1,0:T(8,128)(2,1)} %prototypes_ref.1) | copy-start | bytes 6291460
  100.6 34.1 %copy-start.1 = (f32[8,512]{1,0:T(8,128)S(1)}, f32[8,512]{1,0:T(8,128)}, u32[]{:S(2)}) copy-start(f32[8,512]{1,0:T(8,128)} %get-tuple-element.7) | copy-start | bytes 49156

commit v13 on v11

--- a/solution.py
+++ b/solution.py
@@ -477,13 +477,40 @@
     )(shares)
 
 
+def copy_kernel(rows_ref, protos_ref, image_block, proto_block, image_out, proto_out):
+    image_out[...] = image_block[...]
+    proto_out[...] = proto_block[...]
+
+
+def gather_slots(slots, images, prototypes):
+    block = (None, TILE, E)
+    return pl.pallas_call(
+        copy_kernel,
+        out_shape=(
+            jax.ShapeDtypeStruct((MAXT, TILE, E), images.dtype),
+            jax.ShapeDtypeStruct((MAXT, TILE, E), prototypes.dtype),
+        ),
+        grid_spec=pltpu.PrefetchScalarGridSpec(
+            num_scalar_prefetch=2,
+            grid=(MAXT,),
+            in_specs=[
+                pl.BlockSpec(block, lambda s, rows, protos: (rows[s], 0, 0)),
+                pl.BlockSpec(block, lambda s, rows, protos: (protos[s], 0, 0)),
+            ],
+            out_specs=[
+                pl.BlockSpec(block, lambda s, rows, protos: (s, 0, 0)),
+                pl.BlockSpec(block, lambda s, rows, protos: (s, 0, 0)),
+            ],
+        ),
+    )(slots[0], slots[1], images.reshape(RB_DEV, TILE, E), prototypes.reshape(PB_DEV, TILE, E))
+
+
 def shards(images, prototypes, tile_row, tile_proto, tile_valid):
     img_count = lax.axis_size("img")
     proto_count = lax.axis_size("proto")
     slots = (tile_row.reshape(MAXT), tile_proto.reshape(MAXT), tile_valid.reshape(MAXT))
     log_ratio = math.log(PB_DEV * proto_count / (RB_DEV * img_count))
-    slot_images = images.reshape(RB_DEV, TILE, E)[slots[0]]
-    slot_protos = prototypes.reshape(PB_DEV, TILE, E)[slots[1]]
+    slot_images, slot_protos = gather_slots(slots, images, prototypes)
     row_pot, col_pot, col_columns = sinkhorn(slots, slot_images, slot_protos, log_ratio)
     partial_value = final_pass(slots, images, prototypes, col_columns, row_pot)
     proto_share = scatter_sum(partial_value)

time: 138 us -> 138 us (level); the launches traced: 138 us -> 136 us
  local copies, waits for them, and re-layouts: 7.37 us -> 2.28 us
  Pallas kernels: 129 us -> 134 us
    pallas_call x0 -> x1, Pallas kernels: none -> 5.84 us  [gather_slots(): pl.pallas_call(copy_kernel, out_shape=(jax.ShapeDtypeStruct((MAXT, TILE,...]
    gather x2 -> x0, local copies, waits for them, and re-layouts: 5.08 us -> none  [the longest x1 3.23 us: shards(): slot_images = images.reshape(RB_DEV, TILE, E)[slots[0]]]
where the time goes in v13:
time: 138 us; the launch traced here: 136 us
  Pallas kernels  134 us (97%)
  local copies, waits for them, and re-layouts  2.28 us (2%)
    pallas_call x1, Pallas kernels, sinkhorn(): pl.pallas_call(functools.partial(sinkhorn_kernel, log_ratio), out_shape=(...  87.5 us
    pallas_call x1, Pallas kernels, scatter_sum(): pl.pallas_call(scatter_kernel, out_shape=jax.ShapeDtypeStruct((rows, widt...  34.4 us
    pallas_call x1, Pallas kernels, gather_slots(): pl.pallas_call(copy_kernel, out_shape=(jax.ShapeDtypeStruct((MAXT, TILE,...  5.84 us
    pallas_call x1, Pallas kernels, final_pass(): pl.pallas_call(final_kernel, out_shape=jax.ShapeDtypeStruct((2, PB_DEV, T...  5.76 us

profile of v13, /device:TPU:1, one launch (start us, length us, event | category | flops | bytes accessed | tf_op | source)
XLA Modules:
  0.0 136.5 jit_solution(10958075184489341028)
XLA Ops:
  0.6 5.8 %shard_map.68 = (bf16[6,512,256]{2,1,0:T(8,128)(2,1)}, bf16[6,512,256]{2,1,0:T(8,128)(2,1)}) custom-call(s32[6]{0:T(128)} %bitcast.11, s32[6]{0:T(128)} %bitcast.14, bf16[4,512,256]{2,1,0:T(8,128)(2,1)} %bitcast.8, bf16[8,512,256]{2,1,0:T(8,128)(2,1)} %bitcast.7), custom_call_target="tpu_custom_call" | custom-call | tf_op jit(solution)/shard_map/pallas_call | solution.py:487
  6.5 87.5 %shard_map.69 = (f32[4,1,512]{2,1,0:T(1,128)}, f32[8,512]{1,0:T(8,128)}, f32[8,512,1]{2,1,0:T(8,128)}) custom-call(s32[6]{0:T(128)} %bitcast.12, s32[6]{0:T(128)} %bitcast.15, s32[6]{0:T(128)} %bitcast.17, bf16[6,512,256]{2,1,0:T(8,128)(2,1)} %get-tuple-element.7.images_ref, bf16[6,512,256]{2,1,0:T(8,128)(2,1)} %get-tuple-element.8.prototypes_ref), custom_call_target="tpu_custom_call" | custom-call | tf_op jit(solution)/shard_map/pallas_call | solution.py:359
  94.0 5.8 %shard_map.70.shares_ref = bf16[2,8,256,256]{3,2,1,0:T(8,128)(2,1)} custom-call(s32[6]{0:T(128)} %bitcast.13, s32[6]{0:T(128)} %bitcast.16, s32[6]{0:T(128)} %bitcast.18, bf16[2048,256]{1,0:T(8,128)(2,1)} %images_ref.1, bf16[4096,256]{1,0:T(8,128)(2,1)} %prototypes_ref.1, f32[8,512,1]{2,1,0:T(8,128)} %get-tuple-element.9.col_ref, ...), custom_call_target="tpu_custom_call" | custom-call | tf_op jit(solution)/shard_map/pallas_call | solution.py:190
  99.7 0.0 copy-start
  99.7 34.4 %shard_map.71 = f32[256,256]{1,0:T(8,128)} custom-call(bf16[2,8,256,256]{3,2,1,0:T(8,128)(2,1)} %shard_map.70.shares_ref), custom_call_target="tpu_custom_call" | custom-call | tf_op jit(solution)/shard_map/pallas_call | solution.py:463
  134.2 0.0 copy-done
  134.2 0.6 copy.7
  134.8 1.7 %copy.9 = f32[256,256]{1,0:T(8,128)} copy(f32[256,256]{1,0:T(8,128)} %shard_map.71) | data formatting | bytes 524288
Async XLA Ops:
  99.7 34.5 %copy-start = (f32[8,512]{1,0:T(8,128)S(1)}, f32[8,512]{1,0:T(8,128)}, u32[]{:S(2)}) copy-start(f32[8,512]{1,0:T(8,128)} %get-tuple-element.11) | copy-start | bytes 49156

commit v14 on v11

--- a/solution.py
+++ b/solution.py
@@ -159,7 +159,8 @@
 
 
 def final_kernel(rows_ref, protos_ref, valid_ref, images_ref, prototypes_ref,
-                 col_ref, row_ref, shares_ref, acc_ref):
+                 col_ref, row_ref, col_lanes_ref, shares_ref, col_out, acc_ref):
+    col_out[...] = col_lanes_ref[...]
     acc_ref[...] = jnp.zeros(acc_ref.shape, jnp.float32)
     score_scale = float(E) ** (-0.5)
     for position in range(MAXT):
@@ -186,14 +187,17 @@
             )
 
 
-def final_pass(slots, images, prototypes, col_column, row_pot):
+def final_pass(slots, images, prototypes, col_column, row_pot, col_pot):
     return pl.pallas_call(
         final_kernel,
-        out_shape=jax.ShapeDtypeStruct((2, PB_DEV, TILE // 2, E), jnp.bfloat16),
-        in_specs=slot_specs() + whole_specs(4),
-        out_specs=pl.BlockSpec(memory_space=pltpu.VMEM),
+        out_shape=(
+            jax.ShapeDtypeStruct((2, PB_DEV, TILE // 2, E), jnp.bfloat16),
+            jax.ShapeDtypeStruct(col_pot.shape, col_pot.dtype),
+        ),
+        in_specs=slot_specs() + whole_specs(5),
+        out_specs=tuple(whole_specs(2)),
         scratch_shapes=[pltpu.VMEM((PB_DEV, TILE, E), jnp.float32)],
-    )(*slots, images, prototypes, col_column, row_pot)
+    )(*slots, images, prototypes, col_column, row_pot, col_pot)
 
 
 def to_column(lanes):
@@ -434,12 +438,12 @@
 
     lax.fori_loop(1, chips, send, 0)
     add_pair(chip)
-    out_ref[...] = pair_sums[chip].astype(jnp.float32)
+    out_ref[chip] = pair_sums[chip]
 
     def receive(step, carry):
         source = lax.rem(chip + chips - step, chips)
         peer_copy(source, source).wait_recv()
-        out_ref[...] += landed[source].astype(jnp.float32)
+        out_ref[source] = landed[source]
         return carry
 
     lax.fori_loop(1, chips, receive, 0)
@@ -462,7 +466,7 @@
     half = (chips, rows, width)
     return pl.pallas_call(
         scatter_kernel,
-        out_shape=jax.ShapeDtypeStruct((rows, width), jnp.float32),
+        out_shape=jax.ShapeDtypeStruct(half, shares.dtype),
         in_specs=whole_specs(1),
         out_specs=pl.BlockSpec(memory_space=pltpu.VMEM),
         scratch_shapes=[
@@ -485,8 +489,8 @@
     slot_images = images.reshape(RB_DEV, TILE, E)[slots[0]]
     slot_protos = prototypes.reshape(PB_DEV, TILE, E)[slots[1]]
     row_pot, col_pot, col_columns = sinkhorn(slots, slot_images, slot_protos, log_ratio)
-    partial_value = final_pass(slots, images, prototypes, col_columns, row_pot)
-    proto_share = scatter_sum(partial_value)
+    partial_value, col_pot = final_pass(slots, images, prototypes, col_columns, row_pot, col_pot)
+    proto_share = jnp.sum(scatter_sum(partial_value).astype(jnp.float32), axis=0)
     return (proto_share, col_pot.reshape(PB_DEV * TILE))
 
 

time: 138 us -> 139 us (level)
  other arithmetic: 1.33 us -> 3.42 us
  local copies, waits for them, and re-layouts: 7.37 us -> 5.69 us
    reduce_sum x0 -> x1, other arithmetic: none -> 2.09 us  [shards(): jnp.sum(scatter_sum(partial_value).astype(jnp.float32), axis=0)]
    unnamed x6 -> x5, local copies, waits for them, and re-layouts: 2.29 us -> 0.62 us
where the time goes in v14:
time: 139 us
  Pallas kernels  129 us (93%)
  local copies, waits for them, and re-layouts  5.69 us (4%)
  other arithmetic  3.42 us (2%)
    pallas_call x1, Pallas kernels, sinkhorn(): pl.pallas_call(functools.partial(sinkhorn_kernel, log_ratio), out_shape=(...  88.1 us
    pallas_call x1, Pallas kernels, scatter_sum(): pl.pallas_call(scatter_kernel, out_shape=jax.ShapeDtypeStruct(half, share...  35.7 us
    pallas_call x1, Pallas kernels, final_pass(): pl.pallas_call(final_kernel, out_shape=(jax.ShapeDtypeStruct((2, PB_DEV,...  5.2 us
    gather x1, local copies, waits for them, and re-layouts, shards(): slot_images = images.reshape(RB_DEV, TILE, E)[slots[0]]  3.21 us

profile of v14, /device:TPU:1, one launch (start us, length us, event | category | flops | bytes accessed | tf_op | source)
XLA Modules:
  0.0 138.7 jit_solution(16632135802206708409)
XLA Ops:
  0.6 0.7 fusion
  1.3 0.7 fusion.1
  2.0 0.0 copy-start
  2.0 3.2 %gather_fusion = bf16[6,512,256]{2,1,0:T(8,128)(2,1)} fusion(bf16[4,512,256]{2,1,0:T(8,128)(2,1)} %bitcast.15, s32[1024]{0:T(1024)S(1)} %pad_clamp_fusion.1), kind=kCustom, calls=%fused_computation | custom fusion | bytes 3145752 | tf_op jit(solution)/shard_map/gather | solution.py:489
  5.2 0.0 copy-done
  5.2 1.9 %gather_fusion.1 = bf16[6,512,256]{2,1,0:T(8,128)(2,1)} fusion(bf16[8,512,256]{2,1,0:T(8,128)(2,1)S(1)} %bitcast.16, s32[1024]{0:T(1024)S(1)} %pad_clamp_fusion), kind=kCustom, calls=%fused_computation.1 | custom fusion | bytes 3145752 | tf_op jit(solution)/shard_map/gather | solution.py:490
  7.1 88.1 %shard_map.68 = (f32[4,1,512]{2,1,0:T(1,128)}, f32[8,512]{1,0:T(8,128)}, f32[8,512,1]{2,1,0:T(8,128)}) custom-call(s32[6]{0:T(128)} %bitcast.19, s32[6]{0:T(128)} %bitcast.21, s32[6]{0:T(128)} %bitcast.23, bf16[6,512,256]{2,1,0:T(8,128)(2,1)} %gather_fusion, bf16[6,512,256]{2,1,0:T(8,128)(2,1)} %gather_fusion.1), custom_call_target="tpu_custom_call" | custom-call | tf_op jit(solution)/shard_map/pallas_call | solution.py:363
  95.1 5.2 %shard_map.69 = (bf16[2,8,256,256]{3,2,1,0:T(8,128)(2,1)}, f32[8,512]{1,0:T(8,128)}) custom-call(s32[6]{0:T(128)} %bitcast.20, s32[6]{0:T(128)} %bitcast.22, s32[6]{0:T(128)} %bitcast.24, bf16[2048,256]{1,0:T(8,128)(2,1)} %images_ref.1, bf16[4096,256]{1,0:T(8,128)(2,1)} %prototypes_ref.1, f32[8,512,1]{2,1,0:T(8,128)} %get-tuple-element.7.col_ref, ...), custom_call_target="tpu_custom_call" | custom-call | tf_op jit(solution)/shard_map/pallas_call | solution.py:191
  100.3 0.0 copy-start.1
  100.3 35.7 %shard_map.70 = bf16[8,256,256]{2,1,0:T(8,128)(2,1)} custom-call(bf16[2,8,256,256]{3,2,1,0:T(8,128)(2,1)} %get-tuple-element.10.shares_ref), custom_call_target="tpu_custom_call" | custom-call | tf_op jit(solution)/shard_map/pallas_call | solution.py:467
  136.0 2.1 %convert_reduce_fusion = f32[256,256]{1,0:T(8,128)} fusion(bf16[8,256,256]{2,1,0:T(8,128)(2,1)} %shard_map.70), kind=kLoop, calls=%fused_computation.2 | loop fusion | flops 983040 | bytes 1310720 | tf_op jit(solution)/shard_map/reduce_sum | solution.py:493
  138.1 0.0 copy-done.1
  138.1 0.6 copy.7
  (2 shorter events, 0.0 us)
Async XLA Ops:
  2.0 3.2 %copy-start = (bf16[4096,256]{1,0:T(8,128)(2,1)S(1)}, bf16[4096,256]{1,0:T(8,128)(2,1)}, u32[]{:S(2)}) copy-start(bf16[4096,256]{1,0:T(8,128)(2,1)} %prototypes_ref.1) | copy-start | bytes 6291460
  100.3 37.8 %copy-start.1 = (f32[8,512]{1,0:T(8,128)S(1)}, f32[8,512]{1,0:T(8,128)}, u32[]{:S(2)}) copy-start(f32[8,512]{1,0:T(8,128)} %get-tuple-element.11) | copy-start | bytes 49156

commit v15 on v11

--- a/solution.py
+++ b/solution.py
@@ -324,12 +324,13 @@
 
             lax.fori_loop(1, size, greet, 0)
             greeted += size - 1
-    pl.semaphore_wait(barrier, greeted)
 
     col_t = jnp.zeros((TILE, PB_DEV), jnp.float32)
     for iteration in range(ITERS):
         local = local_merge(True, rows_ref, protos_ref, valid_ref, images_ref, prototypes_ref,
                             col_t)
+        if iteration == 0:
+            pl.semaphore_wait(barrier, greeted)
         merged = exchange("proto", groups["proto"], iteration, local, row_packed,
                           row_refs[0:2], row_refs[2:4], row_refs[4:6])
         row_pot = log_ratio - merged

time: 138 us -> 137 us (level); the launches traced: 138 us -> 136 us
  Pallas kernels: 129 us -> 126 us
    pallas_call x1, Pallas kernels: 88.1 us -> 86.4 us  [sinkhorn(): pl.pallas_call(functools.partial(sinkhorn_kernel, log_ratio), out_shape=(...]
where the time goes in v15:
time: 137 us; the launch traced here: 136 us
  Pallas kernels  126 us (92%)
  local copies, waits for them, and re-layouts  7.37 us (5%)
    pallas_call x1, Pallas kernels, sinkhorn(): pl.pallas_call(functools.partial(sinkhorn_kernel, log_ratio), out_shape=(...  86.4 us
    pallas_call x1, Pallas kernels, scatter_sum(): pl.pallas_call(scatter_kernel, out_shape=jax.ShapeDtypeStruct((rows, widt...  34.9 us
    pallas_call x1, Pallas kernels, final_pass(): pl.pallas_call(final_kernel, out_shape=jax.ShapeDtypeStruct((2, PB_DEV, T...  5.18 us
    gather x1, local copies, waits for them, and re-layouts, shards(): slot_images = images.reshape(RB_DEV, TILE, E)[slots[0]]  3.23 us

profile of v15, /device:TPU:1, one launch (start us, length us, event | category | flops | bytes accessed | tf_op | source)
XLA Modules:
  0.0 135.8 jit_solution(17542978727723538094)
XLA Ops:
  0.6 0.7 fusion
  1.3 0.7 fusion.1
  2.0 0.0 copy-start
  2.0 3.2 %gather_fusion = bf16[6,512,256]{2,1,0:T(8,128)(2,1)} fusion(bf16[4,512,256]{2,1,0:T(8,128)(2,1)} %bitcast.15, s32[1024]{0:T(1024)S(1)} %pad_clamp_fusion.1), kind=kCustom, calls=%fused_computation | custom fusion | bytes 3145752 | tf_op jit(solution)/shard_map/gather | solution.py:486
  5.2 0.0 copy-done
  5.2 1.9 %gather_fusion.1 = bf16[6,512,256]{2,1,0:T(8,128)(2,1)} fusion(bf16[8,512,256]{2,1,0:T(8,128)(2,1)S(1)} %bitcast.16, s32[1024]{0:T(1024)S(1)} %pad_clamp_fusion), kind=kCustom, calls=%fused_computation.1 | custom fusion | bytes 3145752 | tf_op jit(solution)/shard_map/gather | solution.py:487
  7.1 86.4 %shard_map.68 = (f32[4,1,512]{2,1,0:T(1,128)}, f32[8,512]{1,0:T(8,128)}, f32[8,512,1]{2,1,0:T(8,128)}) custom-call(s32[6]{0:T(128)} %bitcast.19, s32[6]{0:T(128)} %bitcast.21, s32[6]{0:T(128)} %bitcast.23, bf16[6,512,256]{2,1,0:T(8,128)(2,1)} %gather_fusion, bf16[6,512,256]{2,1,0:T(8,128)(2,1)} %gather_fusion.1), custom_call_target="tpu_custom_call" | custom-call | tf_op jit(solution)/shard_map/pallas_call | solution.py:360
  93.4 5.2 %shard_map.69.shares_ref = bf16[2,8,256,256]{3,2,1,0:T(8,128)(2,1)} custom-call(s32[6]{0:T(128)} %bitcast.20, s32[6]{0:T(128)} %bitcast.22, s32[6]{0:T(128)} %bitcast.24, bf16[2048,256]{1,0:T(8,128)(2,1)} %images_ref.1, bf16[4096,256]{1,0:T(8,128)(2,1)} %prototypes_ref.1, f32[8,512,1]{2,1,0:T(8,128)} %get-tuple-element.5.col_ref, ...), custom_call_target="tpu_custom_call" | custom-call | tf_op jit(solution)/shard_map/pallas_call | solution.py:190
  98.6 0.0 copy-start.1
  98.6 34.9 %shard_map.70 = f32[256,256]{1,0:T(8,128)} custom-call(bf16[2,8,256,256]{3,2,1,0:T(8,128)(2,1)} %shard_map.69.shares_ref), custom_call_target="tpu_custom_call" | custom-call | tf_op jit(solution)/shard_map/pallas_call | solution.py:464
  133.5 0.0 copy-done.1
  133.5 0.6 copy.7
  134.1 1.7 %copy.9 = f32[256,256]{1,0:T(8,128)} copy(f32[256,256]{1,0:T(8,128)} %shard_map.70) | data formatting | bytes 524288
  (2 shorter events, 0.0 us)
Async XLA Ops:
  2.0 3.2 %copy-start = (bf16[4096,256]{1,0:T(8,128)(2,1)S(1)}, bf16[4096,256]{1,0:T(8,128)(2,1)}, u32[]{:S(2)}) copy-start(bf16[4096,256]{1,0:T(8,128)(2,1)} %prototypes_ref.1) | copy-start | bytes 6291460
  98.6 34.9 %copy-start.1 = (f32[8,512]{1,0:T(8,128)S(1)}, f32[8,512]{1,0:T(8,128)}, u32[]{:S(2)}) copy-start(f32[8,512]{1,0:T(8,128)} %get-tuple-element.7) | copy-start | bytes 49156

commit v16 on v11

--- a/solution.py
+++ b/solution.py
@@ -173,8 +173,9 @@
             products = lax.dot_general(
                 protos_here, rows_here, (((1,), (1,)), ((), ())), preferred_element_type=jnp.float32
             )
+            col_column = pick_column(to_column(col_ref[...]), proto_block, PB_DEV)
             weights = jnp.exp(
-                products * score_scale + col_ref[proto_block] + row_ref[row_block]
+                products * score_scale + col_column + row_ref[row_block]
             ).astype(jnp.bfloat16)
             acc_ref[proto_block] += jnp.dot(weights, rows_here, preferred_element_type=jnp.float32)
 
@@ -343,8 +344,7 @@
     for block in range(RB_DEV):
         row_out[block] = row_pot[block:block + 1]
     col_out[...] = col_pot
-    for block in range(PB_DEV):
-        col_columns_out[block] = col_t[:, block:block + 1]
+    col_columns_out[...] = jnp.zeros(col_columns_out.shape, jnp.float32)
 
 
 def sinkhorn(slots, slot_images, slot_protos, log_ratio):
@@ -361,7 +361,7 @@
         out_shape=(
             jax.ShapeDtypeStruct((RB_DEV, 1, TILE), jnp.float32),
             jax.ShapeDtypeStruct((PB_DEV, TILE), jnp.float32),
-            jax.ShapeDtypeStruct((PB_DEV, TILE, 1), jnp.float32),
+            jax.ShapeDtypeStruct((1, TILE), jnp.float32),
         ),
         in_specs=slot_specs() + whole_specs(2),
         out_specs=tuple(whole_specs(3)),
@@ -485,7 +485,7 @@
     slot_images = images.reshape(RB_DEV, TILE, E)[slots[0]]
     slot_protos = prototypes.reshape(PB_DEV, TILE, E)[slots[1]]
     row_pot, col_pot, col_columns = sinkhorn(slots, slot_images, slot_protos, log_ratio)
-    partial_value = final_pass(slots, images, prototypes, col_columns, row_pot)
+    partial_value = final_pass(slots, images, prototypes, col_pot, row_pot)
     proto_share = scatter_sum(partial_value)
     return (proto_share, col_pot.reshape(PB_DEV * TILE))
 

time: 138 us -> 140 us (1.014)
    pallas_call x1, Pallas kernels: 6.34 us -> 9.03 us  [final_pass(): pl.pallas_call(final_kernel, out_shape=jax.ShapeDtypeStruct((2, PB_DEV, T...]
    pallas_call x1, Pallas kernels: 88.1 us -> 86.6 us  [sinkhorn(): pl.pallas_call(functools.partial(sinkhorn_kernel, log_ratio), out_shape=(...]
    unnamed x6 -> x4, local copies, waits for them, and re-layouts: 2.29 us -> 3 us
where the time goes in v16:
time: 140 us
  Pallas kernels  130 us (93%)
  local copies, waits for them, and re-layouts  8.08 us (6%)
    pallas_call x1, Pallas kernels, sinkhorn(): pl.pallas_call(functools.partial(sinkhorn_kernel, log_ratio), out_shape=(...  86.6 us
    pallas_call x1, Pallas kernels, scatter_sum(): pl.pallas_call(scatter_kernel, out_shape=jax.ShapeDtypeStruct((rows, widt...  34.4 us
    pallas_call x1, Pallas kernels, final_pass(): pl.pallas_call(final_kernel, out_shape=jax.ShapeDtypeStruct((2, PB_DEV, T...  9.03 us
    gather x1, local copies, waits for them, and re-layouts, shards(): slot_images = images.reshape(RB_DEV, TILE, E)[slots[0]]  3.23 us
    unnamed x4, local copies, waits for them, and re-layouts  3 us

profile of v16, /device:TPU:1, one launch (start us, length us, event | category | flops | bytes accessed | tf_op | source)
XLA Modules:
  0.0 140.1 jit_solution(1291878885635919945)
XLA Ops:
  0.6 0.7 fusion
  1.3 0.7 fusion.1
  2.0 0.0 copy-start
  2.0 3.2 %gather_fusion = bf16[6,512,256]{2,1,0:T(8,128)(2,1)} fusion(bf16[4,512,256]{2,1,0:T(8,128)(2,1)} %bitcast.15, s32[1024]{0:T(1024)S(1)} %pad_clamp_fusion.1), kind=kCustom, calls=%fused_computation | custom fusion | bytes 3145752 | tf_op jit(solution)/shard_map/gather | solution.py:485
  5.2 0.0 copy-done
  5.2 1.8 %gather_fusion.1 = bf16[6,512,256]{2,1,0:T(8,128)(2,1)} fusion(bf16[8,512,256]{2,1,0:T(8,128)(2,1)S(1)} %bitcast.16, s32[1024]{0:T(1024)S(1)} %pad_clamp_fusion), kind=kCustom, calls=%fused_computation.1 | custom fusion | bytes 3145752 | tf_op jit(solution)/shard_map/gather | solution.py:486
  7.1 86.6 %shard_map.68 = (f32[4,1,512]{2,1,0:T(1,128)}, f32[8,512]{1,0:T(8,128)}, f32[1,512]{1,0:T(1,128)}) custom-call(s32[6]{0:T(128)} %bitcast.19, s32[6]{0:T(128)} %bitcast.21, s32[6]{0:T(128)} %bitcast.23, bf16[6,512,256]{2,1,0:T(8,128)(2,1)} %gather_fusion, bf16[6,512,256]{2,1,0:T(8,128)(2,1)} %gather_fusion.1), custom_call_target="tpu_custom_call" | custom-call | tf_op jit(solution)/shard_map/pallas_call | solution.py:359
  93.7 1.3 copy.7
  95.0 9.0 %shard_map.69.shares_ref = bf16[2,8,256,256]{3,2,1,0:T(8,128)(2,1)} custom-call(s32[6]{0:T(128)} %bitcast.20, s32[6]{0:T(128)} %bitcast.22, s32[6]{0:T(128)} %bitcast.24, bf16[2048,256]{1,0:T(8,128)(2,1)} %images_ref.1, bf16[4096,256]{1,0:T(8,128)(2,1)} %prototypes_ref.1, f32[8,512]{1,0:T(8,128)} %get-tuple-element.4.col_ref, ...), custom_call_target="tpu_custom_call" | custom-call | tf_op jit(solution)/shard_map/pallas_call | solution.py:191
  104.0 34.4 %shard_map.70 = f32[256,256]{1,0:T(8,128)} custom-call(bf16[2,8,256,256]{3,2,1,0:T(8,128)(2,1)} %shard_map.69.shares_ref), custom_call_target="tpu_custom_call" | custom-call | tf_op jit(solution)/shard_map/pallas_call | solution.py:463
  138.4 1.7 %copy.9 = f32[256,256]{1,0:T(8,128)} copy(f32[256,256]{1,0:T(8,128)} %shard_map.70) | data formatting | bytes 524288
  (2 shorter events, 0.0 us)
Async XLA Ops:
  2.0 3.2 %copy-start = (bf16[4096,256]{1,0:T(8,128)(2,1)S(1)}, bf16[4096,256]{1,0:T(8,128)(2,1)}, u32[]{:S(2)}) copy-start(bf16[4096,256]{1,0:T(8,128)(2,1)} %prototypes_ref.1) | copy-start | bytes 6291460
